TPU v7x, 32 devices: a whole 2x2x4 slice. The times are simulated.
32 devices in a mesh: chan: 8 (over y, x, core), beam: 4 (over z).
Axes of the slice: x: 2, y: 2, z: 4, core: 2. Of those that a mesh axis runs over, the one named last changes fastest.
Arguments:
- observed: bfloat16 [8, 12, 288, 3, 4096], P('beam', None, 'chan'), may hold values from -6 to 6
- beam_pattern: bfloat16 [8, 12, 4096], replicated, may hold values from 0.29882812 to 1
- correction: float32 [8, 288, 2, 3], P('beam', 'chan'), may hold values from -0.5 to 1.3
- block_tile: int32 [8, 12], replicated, may hold values from 0 to 3, as said below
- block_offset: int32 [8, 12], replicated, may hold values from 0 to 19
Outputs:
- faraday: bfloat16 [4, 20, 2, 512, 4096], P('beam', None, None, None, 'chan')
Inputs may be any that keep to these rules, and one draw needn't show every extreme that they name: `block_tile`: group the beams as index j holds them (beams j * 2 to (j + 1) * 2 - 1) and the tiles likewise (tile o for group o). The blocks of the beams of one group lie on the tiles of one group at most 6 times, and exactly 6 times for some tile group, for every beam group.
All inputs are finite; a program needn't handle non-finite values.
Results may differ from a plain program's by a relative error of at most 0.0061.
Values may be sent and summed in bfloat16 or wider, within the bound.
No kernel may reach another device: no remote copies, remote signals or barrier semaphores. Data moves between devices by JAX's collectives and lax.ppermute only.
A program may use at most 128 MiB of HBM per device.

v0:
```python
import jax
import jax.numpy as jnp
from jax import lax
from jax.sharding import PartitionSpec as P

DEPTHS = 512
TILE_DEV = 1
TILE_BLK = 20
CAP = 6


floor_value = 0.25
band_mhz = 288.0
depth_step = 32.0


def faraday_table(channels, depths):
    chan_index = jnp.arange(channels, dtype=jnp.float32)
    frequency = 800.0 + (chan_index + 0.5) * (band_mhz / channels)
    lambda_sq = 299.792458 / frequency * (299.792458 / frequency)
    shifted = lambda_sq - jnp.mean(lambda_sq)
    depth_grid = (jnp.arange(depths, dtype=jnp.float32) - depths // 2) * depth_step
    phase_angle = 2.0 * depth_grid[:, None] * shifted[None, :]
    cosine = jnp.cos(phase_angle)
    sine_part = jnp.sin(phase_angle)
    real_rows = jnp.stack([cosine, sine_part], axis=2).reshape(depths, 2 * channels)
    imag_rows = jnp.stack([-sine_part, cosine], axis=2).reshape(depths, 2 * channels)
    table = jnp.concatenate([real_rows, imag_rows], axis=0) / jnp.sqrt(jnp.float32(channels))
    return table.astype(jnp.bfloat16)


def routing(block_tile, beam_count, blocks_row):
    owner_of = (block_tile // TILE_DEV).reshape(beam_count, blocks_row)
    member = (
        owner_of[:, :, None] == jnp.arange(beam_count, dtype=jnp.int32)[None, None, :]
    ).astype(jnp.int32)
    running = jnp.cumsum(member, axis=1) - member
    rank_in = jnp.sum(running * member, axis=2)
    return (owner_of, rank_in)


def shards(observed, beam_pattern, correction, block_tile, block_offset):
    beam_count = lax.axis_size("beam")
    chan_count = lax.axis_size("chan")
    beam_row = lax.axis_index("beam")
    chan_part = lax.axis_index("chan")
    beam_dev, blk_beam, chan_dev, stokes_in, pixels = observed.shape
    pixel_share = pixels // chan_count
    blocks_row = beam_dev * blk_beam
    capacity = CAP
    local_slots = TILE_DEV * TILE_BLK
    slots_sent = beam_count * capacity
    own_pattern = lax.dynamic_slice_in_dim(beam_pattern, beam_row * beam_dev, beam_dev, 0)
    pattern_wide4 = own_pattern.reshape(beam_dev, blk_beam, 1, chan_count, pixel_share).astype(
        jnp.float32
    )
    split_obs = observed.reshape(beam_dev, blk_beam, chan_dev, stokes_in, chan_count, pixel_share)
    stokes_i = split_obs[:, :, :, 0].astype(jnp.float32)
    stokes_q = split_obs[:, :, :, 1].astype(jnp.float32)
    stokes_u = split_obs[:, :, :, 2].astype(jnp.float32)

    def corrected_row(row):
        first = correction[:, None, :, row, 0][..., None, None]
        second = correction[:, None, :, row, 1][..., None, None]
        third = correction[:, None, :, row, 2][..., None, None]
        return (pattern_wide4 * (first * stokes_i + second * stokes_q + third * stokes_u)).astype(
            jnp.bfloat16
        )

    contrib = jnp.stack([corrected_row(0), corrected_row(1)], axis=4)
    contrib = jnp.transpose(contrib, (3, 0, 1, 2, 4, 5))
    contrib = contrib.reshape(chan_count, blocks_row, chan_dev * 2 * pixel_share)
    owner_of, rank_in = routing(block_tile, beam_count, blocks_row)
    position = owner_of * capacity + rank_in
    my_position = lax.dynamic_index_in_dim(position, beam_row, 0, keepdims=False)
    send_map = (my_position[None, :] == jnp.arange(slots_sent, dtype=jnp.int32)[:, None]).astype(
        jnp.bfloat16
    )
    buffer = jnp.einsum(
        "sb,mbr->smr", send_map, contrib, preferred_element_type=jnp.float32
    ).astype(jnp.bfloat16)
    buffer = buffer.reshape(beam_count, capacity, chan_count, chan_dev, 2, pixel_share)
    slot_local = ((block_tile - beam_row * TILE_DEV) * TILE_BLK + block_offset).reshape(
        beam_count, blocks_row
    )
    mine = owner_of == beam_row
    slot_hits = (
        slot_local[None, :, :] == jnp.arange(local_slots, dtype=jnp.int32)[:, None, None]
    ) & mine[None, :, :]
    rank_hits = rank_in[:, :, None] == jnp.arange(capacity, dtype=jnp.int32)[None, None, :]
    placement_map = jnp.einsum(
        "ljk,jkq->ljq", slot_hits.astype(jnp.float32), rank_hits.astype(jnp.float32)
    )
    placement_map = placement_map.reshape(local_slots, slots_sent).astype(jnp.bfloat16)
    global_slot = (block_tile * TILE_BLK + block_offset).reshape(-1)
    slot_range = beam_row * local_slots + jnp.arange(local_slots, dtype=jnp.int32)
    cover = (global_slot[None, :] == slot_range[:, None]).astype(jnp.float32)
    pattern_wide = beam_pattern.astype(jnp.float32).reshape(-1, pixels)
    squared = pattern_wide * pattern_wide
    received = lax.all_to_all(
        lax.all_to_all(buffer, "beam", split_axis=0, concat_axis=0, tiled=True),
        "chan",
        split_axis=2,
        concat_axis=3,
        tiled=True,
    )
    numerator = jnp.dot(
        placement_map, received.reshape(slots_sent, -1), preferred_element_type=jnp.float32
    )
    numerator = numerator.reshape(local_slots, chan_dev * chan_count, 2, pixel_share)
    squared_share = lax.dynamic_slice_in_dim(squared, chan_part * pixel_share, pixel_share, 1)
    weight_sum = jnp.dot(cover, squared_share, precision=lax.Precision.HIGHEST)
    regrouped = (numerator / jnp.maximum(weight_sum, floor_value)[:, None, None, :]).astype(
        jnp.bfloat16
    )
    channels = regrouped.shape[1]
    pixel_count = regrouped.shape[3]
    kernel = faraday_table(channels, DEPTHS)
    spectrum = jnp.einsum(
        "kx,lxp->lkp",
        kernel,
        regrouped.reshape(local_slots, 2 * channels, pixel_count),
        preferred_element_type=jnp.float32,
    )
    return spectrum.astype(jnp.bfloat16).reshape(TILE_DEV, TILE_BLK, 2, DEPTHS, pixel_count)


def solution(mesh):
    placed = (P("beam", None, "chan", None, None), P(), P("beam", "chan", None, None), P(), P())
    return jax.shard_map(
        shards,
        mesh=mesh,
        in_specs=placed,
        out_specs=P("beam", None, None, None, "chan"),
        check_vma=False,
    )
```

profile of v0, /device:TPU:0, one launch (start us, length us, event | category | flops | bytes accessed | tf_op | source)
XLA Modules:
  0.0 795.9 jit_solution(3652692808522738080)
XLA Ops:
  0.0 46.9 %reshape.300 = bf16[2,12,36,3,8,512]{5,4,0,3,2,1:T(8,128)(2,1)} reshape(bf16[2,12,36,3,4096]{4,0,3,2,1:T(2,128)(2,1)} %param.5) | data formatting | bytes 42467328 | tf_op jit(solution)/shard_map/reshape | solution.py:57
  46.9 0.0 copy-start.2
  46.9 0.0 copy-start
  46.9 20.3 %slice_convert_fusion.2 = (f32[2,12,36,1,8,512]{5,4,0,3,2,1:T(8,128)}, f32[2,12,36,1,8,512]{5,4,0,3,2,1:T(8,128)}, f32[2,12,36,1,8,512]{5,4,0,3,2,1:T(8,128)}) fusion(bf16[2,12,36,3,8,512]{5,4,0,3,2,1:T(8,128)(2,1)} %reshape.300), kind=kLoop, calls=%fused_computation.23 | loop fusion | flops 10616832 | bytes 63700992 | tf_op jit(solution)/shard_map/convert_element_type | solution.py:58
  67.2 0.0 copy-done.2
  67.2 0.0 copy-done
  67.2 0.2 dynamic-slice_convert_fusion
  67.4 0.3 reshape.308
  67.8 16.0 %fusion.2 = (bf16[2,12,36,8,1,512]{5,3,2,1,0,4:T(8,128)(2,1)S(1)}, bf16[2,12,36,8,1,512]{5,3,2,1,0,4:T(8,128)(2,1)S(1)}) fusion(f32[2,12,36,1,8,512]{5,4,0,3,2,1:T(8,128)} %get-tuple-element.8, f32[2,12,36,1,8,512]{5,4,0,3,2,1:T(8,128)} %get-tuple-element.9, f32[2,12,36,1,8,512]{5,4,0,3,2,1:T(8,128)} %get-tuple-element.7, f32[2,36]{1,0:T(2,128)S(1)} %bitcast.77, ...), kind=kLoop, calls=%fused_computation.8 | loop fusion | flops 49545216 | bytes 57018048 | tf_op jit(solution)/shard_map/convert_element_type | solution.py:66
  83.8 1.4 maximum_bitcast_fusion
  85.2 15.2 %copy.74 = bf16[8,2,12,36,2,512]{5,4,3,2,1,0:T(2,128)(2,1)} copy(bf16[8,2,12,36,2,512]{5,0,3,2,1,4:T(8,128)(2,1)S(1)} %maximum_bitcast_fusion) | data formatting | bytes 28311552 | tf_op jit(solution)/shard_map/transpose | solution.py:71
  100.4 0.0 copy-start.1
  100.4 22.3 %reshape.301 = bf16[8,24,36864]{2,1,0:T(8,128)(2,1)} reshape(bf16[8,2,12,36,2,512]{5,4,3,2,1,0:T(2,128)(2,1)} %copy.74) | data formatting | bytes 28311552 | tf_op jit(solution)/shard_map/reshape | solution.py:72
  122.6 0.0 copy-done.1
  122.6 0.1 eq.83
  122.7 0.1 fusion.20
  122.8 0.1 reduce_window_sum.11
  122.8 0.2 select_reduce_fusion
  123.1 14.1 %convolution_convert_fusion = bf16[24,8,36864]{2,0,1:T(8,128)(2,1)} fusion(bf16[8,24,36864]{2,1,0:T(8,128)(2,1)} %reshape.301, s32[24]{0:T(128)S(1)} %fusion.35), kind=kOutput, calls=%fused_computation | convolution fusion | flops 346817088 | bytes 28311648 | tf_op jit(solution)/shard_map/sb,mbr->smr/dot_general | solution.py:79
  137.2 22.4 %reshape.302 = bf16[4,6,8,36,2,512]{5,4,3,1,0,2:T(2,128)(2,1)} reshape(bf16[24,8,36864]{2,0,1:T(8,128)(2,1)} %convolution_convert_fusion) | data formatting | bytes 28311552 | tf_op jit(solution)/shard_map/reshape | solution.py:82
  159.6 13.3 %copy.75 = bf16[4,6,8,36,2,512]{5,4,3,1,2,0:T(2,128)(2,1)S(1)} copy(bf16[4,6,8,36,2,512]{5,4,3,1,0,2:T(2,128)(2,1)} %reshape.302) | data formatting | bytes 28311552 | tf_op jit(solution)/shard_map/reshape | solution.py:82
  172.9 312.9 %all_to_all.14 = bf16[4,6,8,36,2,512]{5,4,3,1,2,0:T(2,128)(2,1)S(1)} all-to-all(bf16[4,6,8,36,2,512]{5,4,3,1,2,0:T(2,128)(2,1)S(1)} %copy.75), channel_id=1, replica_groups=mesh['chan'=8,'beam'=4] {'beam'}, dimensions={0} | all-to-all | bytes 28311552 | tf_op jit(solution)/shard_map/all_to_all | solution.py:101
  485.8 13.0 %copy.76 = bf16[4,6,8,36,2,512]{5,4,3,1,0,2:T(2,128)(2,1)} copy(bf16[4,6,8,36,2,512]{5,4,3,1,2,0:T(2,128)(2,1)S(1)} %all_to_all.14) | data formatting | bytes 28311552 | tf_op jit(solution)/shard_map/all_to_all | solution.py:101
  498.8 0.0 copy-start.3
  498.8 5.6 all-to-all-start.1
  504.4 0.1 convert_multiply_fusion
  504.6 0.9 copy.80
  505.5 1.3 mul.240
  506.9 0.0 copy-done.3
  506.9 0.1 eq.100
  507.0 0.1 eq.90
  507.0 0.1 fusion.17
  507.2 0.7 fusion.33
  508.6 2.1 multiply_sine_fusion
  510.8 0.2 pad_maximum_fusion
  511.0 0.9 copy.82
  511.9 0.8 reshape.306
  512.7 0.9 copy.81
  513.6 0.8 reshape.305
  514.5 1.1 convolution_maximum_fusion
  515.6 144.7 %all-to-all-done.1 = bf16[4,6,8,36,2,512]{5,4,3,1,0,2:T(2,128)(2,1)} async-done(((bf16[4,6,8,36,2,512]{5,4,3,1,0,2:T(2,128)(2,1)}), bf16[4,6,8,36,2,512]{5,4,3,1,0,2:T(2,128)(2,1)}, u32[]{:S(2)}, u32[]{:S(2)}) %all-to-all-start.1) | async-done | bytes 14155808 | tf_op jit(solution)/shard_map/all_to_all | solution.py:100
  660.3 14.4 %copy.77 = bf16[4,6,8,36,2,512]{5,4,3,2,1,0:T(2,128)(2,1)} copy(bf16[4,6,8,36,2,512]{5,4,3,1,0,2:T(2,128)(2,1)} %all-to-all-done.1) | data formatting | bytes 28311552 | tf_op jit(solution)/shard_map/all_to_all | solution.py:100
  674.7 24.3 %reshape.303 = bf16[24,294912]{1,0:T(8,128)(2,1)} reshape(bf16[4,6,8,36,2,512]{5,4,3,2,1,0:T(2,128)(2,1)} %copy.77) | data formatting | bytes 28311552 | tf_op jit(solution)/shard_map/reshape | solution.py:108
  699.0 27.2 %dot_general.22 = bf16[288,2,512,24]{2,1,0,3:T(2,128)(2,1)} reshape(bf16[294912,24]{0,1:T(8,128)(2,1)} %bitcast.74) | data formatting | bytes 28311552 | tf_op jit(solution)/shard_map/dot_general | solution.py:107
  726.2 19.3 %divide_convert_fusion = bf16[20,288,2,512]{3,0,2,1:T(8,128)(2,1)} fusion(f32[20,512]{1,0:T(8,128)S(1)} %convolution_maximum_fusion, bf16[288,2,512,24]{2,1,0,3:T(2,128)(2,1)} %dot_general.22, bf16[20,24]{0,1:T(8,128)(2,1)S(1)} %convert_element_type.119), kind=kOutput, calls=%fused_computation.1 | convolution fusion | flops 294912000 | bytes 25994176 | tf_op jit(solution)/shard_map/dot_general | solution.py:107
  745.4 21.8 %convert_bitcast_fusion = bf16[20,1024,512]{1,2,0:T(8,128)(2,1)} fusion(bf16[20,576,512]{2,0,1:T(8,128)(2,1)} %bitcast.81, f32[512,576]{0,1:T(8,128)S(1)} %reshape.306, f32[512,576]{0,1:T(8,128)S(1)} %reshape.305), kind=kOutput, calls=%fused_computation.2 | convolution fusion | flops 12091850752 | bytes 35127296 | tf_op jit(solution)/shard_map/kx,lxp->lkp/dot_general | solution.py:119
  767.3 28.2 %copy.87 = bf16[20,1024,512]{2,1,0:T(8,128)(2,1)} copy(bf16[20,1024,512]{1,2,0:T(8,128)(2,1)} %convert_bitcast_fusion) | data formatting | bytes 41943040 | tf_op jit(solution)/shard_map/reshape | solution.py:125
  (9 shorter events, 0.1 us)
Async XLA Ops:
  46.9 20.3 %copy-start.2 = (f32[2,36,2,3]{1,2,3,0:T(2,128)S(1)}, f32[2,36,2,3]{1,2,3,0:T(2,128)}, u32[]{:S(2)}) copy-start(f32[2,36,2,3]{1,2,3,0:T(2,128)} %param.7) | copy-start | bytes 5188
  46.9 20.3 %copy-start = (bf16[8,12,4096]{2,0,1:T(8,128)(2,1)S(1)}, bf16[8,12,4096]{2,0,1:T(8,128)(2,1)}, u32[]{:S(2)}) copy-start(bf16[8,12,4096]{2,0,1:T(8,128)(2,1)} %param.6) | copy-start | bytes 2359300
  100.4 22.3 %copy-start.1 = (s32[8,12]{1,0:T(8,128)S(1)}, s32[8,12]{1,0:T(8,128)}, u32[]{:S(2)}) copy-start(s32[8,12]{1,0:T(8,128)} %param.8) | copy-start | bytes 1156
  498.8 8.1 %copy-start.3 = (s32[8,12]{1,0:T(8,128)S(1)}, s32[8,12]{1,0:T(8,128)}, u32[]{:S(2)}) copy-start(s32[8,12]{1,0:T(8,128)} %param.9) | copy-start | bytes 1156
  498.8 161.5 %all-to-all-start.1 = ((bf16[4,6,8,36,2,512]{5,4,3,1,0,2:T(2,128)(2,1)}), bf16[4,6,8,36,2,512]{5,4,3,1,0,2:T(2,128)(2,1)}, u32[]{:S(2)}, u32[]{:S(2)}) async-start(bf16[4,6,8,36,2,512]{5,4,3,1,0,2:T(2,128)(2,1)} %copy.76), calls=%async_computation.1 | async-start | bytes 28311552 | tf_op jit(solution)/shard_map/all_to_all | solution.py:100
where the time goes:
time: 808 us; the launch traced here: 796 us
  blocking collectives  313 us (39%)
  local copies, waits for them, and re-layouts  233 us (29%)
  waiting for transfers between devices  145 us (18%)
  matrix products  56.5 us (7%)
  other arithmetic  41.5 us (5%)
    all_to_all x1, blocking collectives, shards(): lax.all_to_all(buffer, 'beam', split_axis=0, concat_axis=0, tiled=True)  313 us
    all_to_all x1, waiting for transfers between devices, shards(): lax.all_to_all(lax.all_to_all(buffer, 'beam', split_axis=0, concat_axis=0...  145 us
    reshape x1, local copies, waits for them, and re-layouts, shards(): observed.reshape(beam_dev, blk_beam, chan_dev, stokes_in, chan_count, pix...  46.9 us
    reshape x2, local copies, waits for them, and re-layouts, shards(): buffer.reshape(beam_count, capacity, chan_count, chan_dev, 2, pixel_share)  35.6 us
    reshape x1, local copies, waits for them, and re-layouts, shards(): spectrum.astype(jnp.bfloat16)  28.2 us
    dot_general x1, local copies, waits for them, and re-layouts, shards(): jnp.dot(placement_map, received.reshape(slots_sent, -1), preferred_elemen...  27.2 us
    reshape x1, local copies, waits for them, and re-layouts, shards(): received.reshape(slots_sent, -1)  24.3 us
    reshape x1, local copies, waits for them, and re-layouts, shards(): contrib.reshape(chan_count, blocks_row, chan_dev * 2 * pixel_share)  22.3 us
  transfers between devices with their start and end apart: 1, of which 1 were waited for; matrix products, arithmetic and copies ran while one was open for 1% of the time, Pallas kernels for 0%

commit v1 on v0

v1 whole, which is shorter than its diff:
```python
import functools

import jax
import jax.numpy as jnp
from jax import lax
from jax.experimental import pallas as pl
from jax.experimental.pallas import tpu as pltpu
from jax.sharding import PartitionSpec as P

DEPTHS = 512
TILE_DEV = 1
TILE_BLK = 20
CAP = 6
LANES = 128


floor_value = 0.25
band_mhz = 288.0
depth_step = 32.0


def faraday_table(channels, depths):
    chan_index = jnp.arange(channels, dtype=jnp.float32)
    frequency = 800.0 + (chan_index + 0.5) * (band_mhz / channels)
    lambda_sq = 299.792458 / frequency * (299.792458 / frequency)
    shifted = lambda_sq - jnp.mean(lambda_sq)
    depth_grid = (jnp.arange(depths, dtype=jnp.float32) - depths // 2) * depth_step
    phase_angle = 2.0 * depth_grid[:, None] * shifted[None, :]
    cosine = jnp.cos(phase_angle)
    sine_part = jnp.sin(phase_angle)
    real_rows = jnp.stack([cosine, sine_part], axis=2).reshape(depths, 2 * channels)
    imag_rows = jnp.stack([-sine_part, cosine], axis=2).reshape(depths, 2 * channels)
    table = jnp.concatenate([real_rows, imag_rows], axis=0) / jnp.sqrt(jnp.float32(channels))
    return table.astype(jnp.bfloat16)


def routing(block_tile, beam_count, blocks_row):
    owner_of = (block_tile // TILE_DEV).reshape(beam_count, blocks_row)
    earlier = jnp.arange(blocks_row)[None, :] < jnp.arange(blocks_row)[:, None]
    same = owner_of[:, :, None] == owner_of[:, None, :]
    rank_in = jnp.sum((same & earlier[None]).astype(jnp.int32), axis=2)
    return (owner_of, rank_in)


def send_body(chan_count, blk_beam, owner_s, rank_s, *refs):
    obs_refs = refs[:chan_count]
    mix_ref, pattern_ref, out_ref = refs[chan_count:]
    rows = out_ref.shape[3]
    mix = mix_ref[0]
    for part in range(chan_count):
        pixels = obs_refs[part][0].reshape(-1, LANES)
        both = jnp.dot(mix, pixels, preferred_element_type=jnp.float32)
        corrected = both[:rows] + both[rows:]
        out_ref[0, part, 0] = (corrected * pattern_ref[0, part : part + 1]).astype(out_ref.dtype)


def send_chunk(obs_t, mix, pattern, owner, rank, chunk, beam_count, chan_count):
    blk_beam, chan_dev, stokes_in, beam_dev, pixels = obs_t.shape
    tiles = pixels // chan_count // LANES
    rows = chan_dev * 2
    obs_specs = [
        pl.BlockSpec(
            (1, chan_dev, stokes_in, beam_dev, LANES),
            lambda k, d, owner_s, rank_s, part=part: (k, 0, 0, 0, part * tiles + chunk),
        )
        for part in range(chan_count)
    ]
    return pl.pallas_call(
        functools.partial(send_body, chan_count, blk_beam),
        out_shape=jax.ShapeDtypeStruct((beam_count, chan_count, CAP, rows, LANES), jnp.bfloat16),
        grid_spec=pltpu.PrefetchScalarGridSpec(
            num_scalar_prefetch=2,
            grid=(blk_beam, beam_dev),
            in_specs=obs_specs
            + [
                pl.BlockSpec((1,) + mix.shape[1:], lambda k, d, owner_s, rank_s: (d, 0, 0)),
                pl.BlockSpec(
                    (1, chan_count, LANES), lambda k, d, owner_s, rank_s: (d * blk_beam + k, 0, 0)
                ),
            ],
            out_specs=pl.BlockSpec(
                (1, chan_count, 1, rows, LANES),
                lambda k, d, owner_s, rank_s: (
                    owner_s[d * blk_beam + k],
                    0,
                    rank_s[d * blk_beam + k],
                    0,
                    0,
                ),
            ),
        ),
        name=f"send_chunk_{chunk}",
    )(owner, rank, *([obs_t] * chan_count), mix, pattern)


def sky_body(pair, order_s, start_s, recv_ref, inverse_ref, table_ref, *refs):
    out_ref, total = refs[-2:]
    step = pl.program_id(0)
    parts, rows = recv_ref.shape[1], recv_ref.shape[3]
    total[...] = jnp.zeros_like(total)
    for side in range(pair):
        slot = step * pair + side

        def add(i, carry):
            source, rank = order_s[0, i], order_s[1, i]
            for part in range(parts):
                total[part * rows : (part + 1) * rows, side * LANES : (side + 1) * LANES] += recv_ref[
                    source, part, rank
                ].astype(jnp.float32)
            return carry

        lax.fori_loop(start_s[slot], start_s[slot + 1], add, 0)
    sky = jnp.concatenate(
        [
            total[:, side * LANES : (side + 1) * LANES] * inverse_ref[pl.ds(step * pair + side, 1)]
            for side in range(pair)
        ],
        axis=1,
    ).astype(jnp.bfloat16)
    spectrum = jnp.dot(table_ref[...], sky, preferred_element_type=jnp.float32)
    for side in range(pair):
        out_ref[side] = spectrum[:, side * LANES : (side + 1) * LANES].astype(out_ref.dtype)


def sky_chunk(recv, inverse, table, order, start, chunk, tiles, earlier):
    pair = 2
    slots = inverse.shape[0]
    whole = lambda a: pl.BlockSpec(a.shape, lambda l, *s: (0,) * a.ndim)
    in_specs = [whole(recv), whole(inverse), whole(table)]
    args = [order, start, recv, inverse, table]
    aliases = {}
    if earlier is not None:
        in_specs.append(pl.BlockSpec(memory_space=pl.ANY))
        aliases = {len(args): 0}
        args.append(earlier)
    return pl.pallas_call(
        functools.partial(sky_body, pair),
        out_shape=jax.ShapeDtypeStruct((slots, table.shape[0], tiles * LANES), jnp.bfloat16),
        grid_spec=pltpu.PrefetchScalarGridSpec(
            num_scalar_prefetch=2,
            grid=(slots // pair,),
            in_specs=in_specs,
            out_specs=pl.BlockSpec((pair, table.shape[0], LANES), lambda l, *s: (l, 0, chunk)),
            scratch_shapes=[pltpu.VMEM((table.shape[1], pair * LANES), jnp.float32)],
        ),
        input_output_aliases=aliases,
        compiler_params=pltpu.CompilerParams(vmem_limit_bytes=40 << 20),
        name=f"sky_chunk_{chunk}",
    )(*args)


def shards(observed, beam_pattern, correction, block_tile, block_offset):
    beam_count = lax.axis_size("beam")
    chan_count = lax.axis_size("chan")
    beam_row = lax.axis_index("beam")
    chan_part = lax.axis_index("chan")
    beam_dev, blk_beam, chan_dev, stokes_in, pixels = observed.shape
    pixel_share = pixels // chan_count
    tiles = pixel_share // LANES
    blocks_row = beam_dev * blk_beam
    local_slots = TILE_DEV * TILE_BLK
    rows = chan_dev * 2

    owner_of, rank_in = routing(block_tile, beam_count, blocks_row)
    my_owner = lax.dynamic_index_in_dim(owner_of, beam_row, 0, keepdims=False)
    my_rank = lax.dynamic_index_in_dim(rank_in, beam_row, 0, keepdims=False)

    same_chan = jnp.eye(chan_dev, dtype=jnp.float32)
    same_beam = jnp.eye(beam_dev, dtype=jnp.float32)
    mix = (
        correction[:, :, :, None, :, None]
        * same_chan[None, :, None, :, None, None]
        * same_beam[:, None, None, None, None, :]
    ).reshape(beam_dev, rows, chan_dev * stokes_in * beam_dev)
    mix_high = mix.astype(jnp.bfloat16)
    mix_low = (mix - mix_high.astype(jnp.float32)).astype(jnp.bfloat16)
    mix = jnp.concatenate([mix_high, mix_low], axis=1)

    own_pattern = lax.dynamic_slice_in_dim(beam_pattern, beam_row * beam_dev, beam_dev, 0)
    own_pattern = own_pattern.astype(jnp.float32).reshape(blocks_row, chan_count, tiles, LANES)
    obs_t = jnp.transpose(observed, (1, 2, 3, 0, 4))

    slot_of = (block_tile % TILE_DEV * TILE_BLK + block_offset).reshape(beam_count, blocks_row)
    mine = owner_of == beam_row
    ranks = jnp.arange(CAP, dtype=jnp.int32)
    hit = mine[:, :, None] & (rank_in[:, :, None] == ranks[None, None, :])
    entry_slot = jnp.min(jnp.where(hit, slot_of[:, :, None], local_slots), axis=1).reshape(-1)
    entries = beam_count * CAP
    index = jnp.arange(entries, dtype=jnp.int32)
    before = (entry_slot[None, :] < entry_slot[:, None]) | (
        (entry_slot[None, :] == entry_slot[:, None]) & (index[None, :] < index[:, None])
    )
    place = jnp.sum(before.astype(jnp.int32), axis=1)
    order = jnp.sum(jnp.where(place[None, :] == index[:, None], index[None, :], 0), axis=1)
    order = jnp.stack([order // CAP, order % CAP])
    slot_index = jnp.arange(local_slots + 1, dtype=jnp.int32)
    start = jnp.sum((entry_slot[None, :] < slot_index[:, None]).astype(jnp.int32), axis=1)

    global_slot = (block_tile * TILE_BLK + block_offset).reshape(-1)
    slot_range = beam_row * local_slots + jnp.arange(local_slots, dtype=jnp.int32)
    cover = (global_slot[None, :] == slot_range[:, None]).astype(jnp.float32)
    share = lax.dynamic_slice_in_dim(beam_pattern, chan_part * pixel_share, pixel_share, 2)
    share = share.astype(jnp.float32).reshape(-1, pixel_share)
    weight_sum = jnp.dot(cover, share * share, precision=lax.Precision.HIGHEST)
    inverse = 1.0 / jnp.maximum(weight_sum, floor_value)
    table = faraday_table(chan_dev * chan_count, DEPTHS)

    spectrum = None
    for chunk in range(tiles):
        sent = send_chunk(
            obs_t, mix, own_pattern[:, :, chunk], my_owner, my_rank, chunk, beam_count, chan_count
        )
        received = lax.all_to_all(
            sent.reshape((beam_count * chan_count,) + sent.shape[2:]),
            ("beam", "chan"),
            split_axis=0,
            concat_axis=0,
            tiled=True,
        ).reshape(sent.shape)
        spectrum = sky_chunk(
            received,
            inverse[:, chunk * LANES : (chunk + 1) * LANES],
            table,
            order,
            start,
            chunk,
            tiles,
            spectrum,
        )
    return spectrum.reshape(TILE_DEV, TILE_BLK, 2, DEPTHS, pixel_share)


def solution(mesh):
    placed = (P("beam", None, "chan", None, None), P(), P("beam", "chan", None, None), P(), P())
    return jax.shard_map(
        shards,
        mesh=mesh,
        in_specs=placed,
        out_specs=P("beam", None, None, None, "chan"),
        check_vma=False,
    )
```

time: 808 us -> 394 us (0.49)
  blocking collectives: 313 us -> 0 us
  local copies, waits for them, and re-layouts: 233 us -> 28.7 us
  Pallas kernels: 0 us -> 125 us
  waiting for transfers between devices: 145 us -> 206 us
  matrix products: 56.5 us -> 0.23 us
  other arithmetic: 41.5 us -> 8.78 us
  starting transfers between devices: 5.64 us -> 19.7 us
    all_to_all x1 -> x0, blocking collectives: 313 us -> none  [shards(): lax.all_to_all(buffer, 'beam', split_axis=0, concat_axis=0, tiled=True)]
    reshape x6 -> x2, local copies, waits for them, and re-layouts: 157 us -> 0.34 us  [the longest x1 0.26 us: shards(): own_pattern.astype(jnp.float32)]
    pallas_call x0 -> x8, Pallas kernels: none -> 125 us  [the longest x4 85.3 us: send_chunk(): pl.pallas_call(functools.partial(send_body, chan_count, blk_beam), out_sh...]
    all_to_all x1 -> x4, waiting for transfers between devices: 145 us -> 206 us  [shards(): lax.all_to_all(sent.reshape((beam_count * chan_count,) + sent.shape[2:]),...]
    dot_general x5 -> x1, matrix products: 56.5 us -> 0.23 us  [shards(): weight_sum = jnp.dot(cover, share * share, precision=lax.Precision.HIGHEST)]
    convert_element_type x4, other arithmetic: 36.6 us -> 1.84 us  [the longest x1 1.81 us: faraday_table(): return table.astype(jnp.bfloat16)]
    all_to_all x2 -> x0, local copies, waits for them, and re-layouts: 27.4 us -> none  [the longest x1 14.4 us: shards(): lax.all_to_all(lax.all_to_all(buffer, 'beam', split_axis=0, concat_axis=0...]
    dot_general x1 -> x0, local copies, waits for them, and re-layouts: 27.2 us -> none  [shards(): jnp.dot(placement_map, received.reshape(slots_sent, -1), preferred_elemen...]
  transfers between devices with their start and end apart: 1 -> 4, of which waited for: 1 -> 4; matrix products, arithmetic and copies ran while one was open for 1% -> 5% of each run, Pallas kernels for 0% -> 24%
where the time goes in v1:
time: 394 us; the launch traced here: 390 us
  waiting for transfers between devices  206 us (52%)
  Pallas kernels  125 us (32%)
  local copies, waits for them, and re-layouts  28.7 us (7%)
  starting transfers between devices  19.7 us (5%)
  other arithmetic  8.78 us (2%)
    all_to_all x4, waiting for transfers between devices, shards(): lax.all_to_all(sent.reshape((beam_count * chan_count,) + sent.shape[2:]),...  206 us
    pallas_call x4, Pallas kernels, send_chunk(): pl.pallas_call(functools.partial(send_body, chan_count, blk_beam), out_sh...  85.3 us
    pallas_call x4, Pallas kernels, sky_chunk(): pl.pallas_call(functools.partial(sky_body, pair), out_shape=jax.ShapeDtyp...  40 us
    all_to_all x4, starting transfers between devices, shards(): lax.all_to_all(sent.reshape((beam_count * chan_count,) + sent.shape[2:]),...  19.7 us
    mul x5, local copies, waits for them, and re-layouts, shards(): correction[:, :, :, None, :, None] * same_chan[None, :, None, :, None, None]  9.92 us
  transfers between devices with their start and end apart: 4, of which 4 were waited for; matrix products, arithmetic and copies ran while one was open for 5% of the time, Pallas kernels for 24%

profile of v1, /device:TPU:0, one launch (start us, length us, event | category | flops | bytes accessed | tf_op | source)
XLA Modules:
  0.0 389.8 jit_solution(8222346622655377538)
XLA Ops:
  0.0 1.4 constant_dynamic-slice_fusion
  1.4 0.1 copy_convert_fusion
  1.5 0.3 reshape.310
  1.8 1.0 fusion.12
  2.9 0.1 copy.32
  3.1 0.4 broadcast_multiply_fusion
  3.4 4.1 %mul.112 = f32[2,36,2,36,3,2]{2,1,5,4,3,0:T(8,128)} broadcast(f32[2,36,2,36,3]{2,1,4,3,0:T(8,128)S(1)} %broadcast_multiply_fusion), dimensions={0,1,2,3,4} | broadcast | bytes 186624 | tf_op jit(solution)/shard_map/mul | solution.py:171
  7.5 5.5 %mul.113 = f32[2,72,216]{1,2,0:T(8,128)S(1)} reshape(f32[2,36,2,36,3,2]{2,1,5,4,3,0:T(8,128)} %mul.112) | data formatting | bytes 248832 | tf_op jit(solution)/shard_map/mul | solution.py:171
  13.1 0.1 copy.33
  13.2 0.1 mul.115
  13.4 0.2 convert_reduce_fusion
  13.6 0.6 fusion.10
  14.2 0.7 pad_maximum_fusion.2.refs_8_
  14.9 21.3 %send_chunk_0.1 = bf16[4,8,6,72,128]{4,3,2,1,0:T(8,128)(2,1)} custom-call(s32[24]{0:T(128)} %get-tuple-element.22.owner_s, s32[24]{0:T(128)} %get-tuple-element.23.rank_s, bf16[12,36,3,2,4096]{4,3,2,1,0:T(2,128)(2,1)} %bitcast.44, bf16[12,36,3,2,4096]{4,3,2,1,0:T(2,128)(2,1)} %bitcast.45, bf16[12,36,3,2,4096]{4,3,2,1,0:T(2,128)(2,1)} %bitcast.46, ...), custom_call_target="tpu_custom_call" | custom-call | tf_op jit(solution)/shard_map/send_chunk_0/pallas_call | solution.py:68
  36.2 7.3 %all-to-all-start.3 = ((bf16[32,6,72,128]{3,2,1,0:T(8,128)(2,1)}), bf16[32,6,72,128]{3,2,1,0:T(8,128)(2,1)S(1)}, u32[]{:S(2)}, u32[]{:S(2)}) async-start(bf16[32,6,72,128]{3,2,1,0:T(8,128)(2,1)} %bitcast.79), calls=%async_computation.3 | async-start | bytes 7077888 | tf_op jit(solution)/shard_map/all_to_all | solution.py:213
  43.5 21.3 %send_chunk_1.1 = bf16[4,8,6,72,128]{4,3,2,1,0:T(8,128)(2,1)} custom-call(s32[24]{0:T(128)} %get-tuple-element.22.owner_s, s32[24]{0:T(128)} %get-tuple-element.23.rank_s, bf16[12,36,3,2,4096]{4,3,2,1,0:T(2,128)(2,1)} %bitcast.59, bf16[12,36,3,2,4096]{4,3,2,1,0:T(2,128)(2,1)} %bitcast.53, bf16[12,36,3,2,4096]{4,3,2,1,0:T(2,128)(2,1)} %bitcast.54, ...), custom_call_target="tpu_custom_call" | custom-call | tf_op jit(solution)/shard_map/send_chunk_1/pallas_call | solution.py:68
  64.9 58.5 %all-to-all-done.3 = bf16[32,6,72,128]{3,2,1,0:T(8,128)(2,1)S(1)} async-done(((bf16[32,6,72,128]{3,2,1,0:T(8,128)(2,1)}), bf16[32,6,72,128]{3,2,1,0:T(8,128)(2,1)S(1)}, u32[]{:S(2)}, u32[]{:S(2)}) %all-to-all-start.3) | async-done | bytes 3538976 | tf_op jit(solution)/shard_map/all_to_all | solution.py:213
  123.4 1.7 copy-done.2
  125.1 4.0 %all-to-all-start.2 = ((bf16[32,6,72,128]{3,2,1,0:T(8,128)(2,1)}), bf16[32,6,72,128]{3,2,1,0:T(8,128)(2,1)S(1)}, u32[]{:S(2)}, u32[]{:S(2)}) async-start(bf16[32,6,72,128]{3,2,1,0:T(8,128)(2,1)} %bitcast.78), calls=%async_computation.2 | async-start | bytes 7077888 | tf_op jit(solution)/shard_map/all_to_all | solution.py:213
  129.1 21.3 %send_chunk_2.1 = bf16[4,8,6,72,128]{4,3,2,1,0:T(8,128)(2,1)} custom-call(s32[24]{0:T(128)} %get-tuple-element.22.owner_s, s32[24]{0:T(128)} %get-tuple-element.23.rank_s, bf16[12,36,3,2,4096]{4,3,2,1,0:T(2,128)(2,1)} %bitcast.60, bf16[12,36,3,2,4096]{4,3,2,1,0:T(2,128)(2,1)} %bitcast.61, bf16[12,36,3,2,4096]{4,3,2,1,0:T(2,128)(2,1)} %bitcast.62, ...), custom_call_target="tpu_custom_call" | custom-call | tf_op jit(solution)/shard_map/send_chunk_2/pallas_call | solution.py:68
  150.4 58.5 %all-to-all-done.2 = bf16[32,6,72,128]{3,2,1,0:T(8,128)(2,1)S(1)} async-done(((bf16[32,6,72,128]{3,2,1,0:T(8,128)(2,1)}), bf16[32,6,72,128]{3,2,1,0:T(8,128)(2,1)S(1)}, u32[]{:S(2)}, u32[]{:S(2)}) %all-to-all-start.2) | async-done | bytes 3538976 | tf_op jit(solution)/shard_map/all_to_all | solution.py:213
  208.9 1.9 copy-done
  210.8 4.1 %all-to-all-start.1 = ((bf16[32,6,72,128]{3,2,1,0:T(8,128)(2,1)}), bf16[32,6,72,128]{3,2,1,0:T(8,128)(2,1)}, u32[]{:S(2)}, u32[]{:S(2)}) async-start(bf16[32,6,72,128]{3,2,1,0:T(8,128)(2,1)} %bitcast.77), calls=%async_computation.1 | async-start | bytes 7077888 | tf_op jit(solution)/shard_map/all_to_all | solution.py:213
  214.9 21.4 %send_chunk_3.1 = bf16[4,8,6,72,128]{4,3,2,1,0:T(8,128)(2,1)} custom-call(s32[24]{0:T(128)} %get-tuple-element.22.owner_s, s32[24]{0:T(128)} %get-tuple-element.23.rank_s, bf16[12,36,3,2,4096]{4,3,2,1,0:T(2,128)(2,1)} %bitcast.68, bf16[12,36,3,2,4096]{4,3,2,1,0:T(2,128)(2,1)} %bitcast.69, bf16[12,36,3,2,4096]{4,3,2,1,0:T(2,128)(2,1)} %bitcast.70, ...), custom_call_target="tpu_custom_call" | custom-call | tf_op jit(solution)/shard_map/send_chunk_3/pallas_call | solution.py:68
  236.3 58.4 %all-to-all-done.1 = bf16[32,6,72,128]{3,2,1,0:T(8,128)(2,1)} async-done(((bf16[32,6,72,128]{3,2,1,0:T(8,128)(2,1)}), bf16[32,6,72,128]{3,2,1,0:T(8,128)(2,1)}, u32[]{:S(2)}, u32[]{:S(2)}) %all-to-all-start.1) | async-done | bytes 3538976 | tf_op jit(solution)/shard_map/all_to_all | solution.py:213
  294.7 4.3 %all-to-all-start = ((bf16[32,6,72,128]{3,2,1,0:T(8,128)(2,1)}), bf16[32,6,72,128]{3,2,1,0:T(8,128)(2,1)}, u32[]{:S(2)}, u32[]{:S(2)}) async-start(bf16[32,6,72,128]{3,2,1,0:T(8,128)(2,1)} %bitcast.76), calls=%async_computation | async-start | bytes 7077888 | tf_op jit(solution)/shard_map/all_to_all | solution.py:213
  299.1 0.2 select_reduce_fusion.1
  299.5 0.9 convert_multiply_fusion
  300.4 0.1 copy.36
  300.7 0.6 fusion.9
  302.0 2.1 multiply_sine_fusion
  304.1 1.2 pad_maximum_fusion
  305.4 0.9 copy.37
  306.3 1.9 reshape.300
  308.1 1.7 copy.39
  309.8 2.2 copy.38
  312.0 1.9 reshape.301
  313.9 2.7 copy.40
  316.6 0.2 convert_reduce_fusion.2
  316.8 0.1 select_reduce_fusion
  316.9 0.1 convert_reduce_fusion.1.start_s
  317.1 1.8 fusion.table_ref
  318.9 0.2 fusion.1
  319.1 9.0 %sky_chunk_0.1.refs_0_ = bf16[20,1024,512]{2,1,0:T(8,128)(2,1)} custom-call(s32[2,24]{1,0:T(2,128)S(1)} %pad_add_fusion.order_s, s32[21]{0:T(128)S(1)} %convert_reduce_fusion.1.start_s, bf16[4,8,6,72,128]{4,3,2,1,0:T(8,128)(2,1)S(1)} %bitcast.43, f32[20,128]{1,0:T(8,128)S(1)} %get-tuple-element.13.inverse_ref, bf16[1024,576]{1,0:T(8,128)(2,1)S(1)} %fusion.table_ref), custom_call_target="tpu_custom_call" | custom-call | tf_op jit(solution)/shard_map/sky_chunk_0/pallas_call | solution.py:136
  328.1 9.0 %sky_chunk_1.1.refs_0_ = bf16[20,1024,512]{2,1,0:T(8,128)(2,1)} custom-call(s32[2,24]{1,0:T(2,128)S(1)} %pad_add_fusion.order_s, s32[21]{0:T(128)S(1)} %convert_reduce_fusion.1.start_s, bf16[4,8,6,72,128]{4,3,2,1,0:T(8,128)(2,1)S(1)} %bitcast.42, f32[20,128]{1,0:T(8,128)S(1)} %get-tuple-element.14.inverse_ref, ...), custom_call_target="tpu_custom_call", output_to_operand_aliasing={{}: (5, {})} | custom-call | tf_op jit(solution)/shard_map/sky_chunk_1/pallas_call | solution.py:136
  337.1 11.0 %sky_chunk_2.1.refs_0_ = bf16[20,1024,512]{2,1,0:T(8,128)(2,1)} custom-call(s32[2,24]{1,0:T(2,128)S(1)} %pad_add_fusion.order_s, s32[21]{0:T(128)S(1)} %convert_reduce_fusion.1.start_s, bf16[4,8,6,72,128]{4,3,2,1,0:T(8,128)(2,1)} %bitcast.11.recv_ref, f32[20,128]{1,0:T(8,128)S(1)} %get-tuple-element.15.inverse_ref, ...), custom_call_target="tpu_custom_call", output_to_operand_aliasing={{}: (5, {})} | custom-call | tf_op jit(solution)/shard_map/sky_chunk_2/pallas_call | solution.py:136
  348.1 30.7 %all-to-all-done = bf16[32,6,72,128]{3,2,1,0:T(8,128)(2,1)} async-done(((bf16[32,6,72,128]{3,2,1,0:T(8,128)(2,1)}), bf16[32,6,72,128]{3,2,1,0:T(8,128)(2,1)}, u32[]{:S(2)}, u32[]{:S(2)}) %all-to-all-start) | async-done | bytes 3538976 | tf_op jit(solution)/shard_map/all_to_all | solution.py:213
  378.8 11.0 %sky_chunk_3.1 = bf16[20,1024,512]{2,1,0:T(8,128)(2,1)} custom-call(s32[2,24]{1,0:T(2,128)S(1)} %pad_add_fusion.order_s, s32[21]{0:T(128)S(1)} %convert_reduce_fusion.1.start_s, bf16[4,8,6,72,128]{4,3,2,1,0:T(8,128)(2,1)} %bitcast.8.recv_ref, f32[20,128]{1,0:T(8,128)S(1)} %get-tuple-element.16.inverse_ref, ...), custom_call_target="tpu_custom_call", output_to_operand_aliasing={{}: (5, {})} | custom-call | tf_op jit(solution)/shard_map/sky_chunk_3/pallas_call | solution.py:136
  (41 shorter events, 0.6 us)
Async XLA Ops:
  0.0 2.8 copy-start.7
  0.0 2.9 copy-start.11
  2.9 10.7 %copy-start.4 = (s32[4,24]{1,0:T(4,128)}, s32[4,24]{1,0:T(4,128)S(1)}, u32[]{:S(2)}) copy-start(s32[4,24]{1,0:T(4,128)S(1)} %reshape.295) | copy-start | bytes 1156
  13.6 22.6 %copy-start.9 = (s32[4,24]{1,0:T(4,128)}, s32[4,24]{1,0:T(4,128)S(1)}, u32[]{:S(2)}) copy-start(s32[4,24]{1,0:T(4,128)S(1)} %convert_reduce_fusion) | copy-start | bytes 1156
  36.2 87.1 %all-to-all-start.3 = ((bf16[32,6,72,128]{3,2,1,0:T(8,128)(2,1)}), bf16[32,6,72,128]{3,2,1,0:T(8,128)(2,1)S(1)}, u32[]{:S(2)}, u32[]{:S(2)}) async-start(bf16[32,6,72,128]{3,2,1,0:T(8,128)(2,1)} %bitcast.79), calls=%async_computation.3 | async-start | bytes 7077888 | tf_op jit(solution)/shard_map/all_to_all | solution.py:213
  123.4 1.7 copy-start.2
  125.1 83.8 %all-to-all-start.2 = ((bf16[32,6,72,128]{3,2,1,0:T(8,128)(2,1)}), bf16[32,6,72,128]{3,2,1,0:T(8,128)(2,1)S(1)}, u32[]{:S(2)}, u32[]{:S(2)}) async-start(bf16[32,6,72,128]{3,2,1,0:T(8,128)(2,1)} %bitcast.78), calls=%async_computation.2 | async-start | bytes 7077888 | tf_op jit(solution)/shard_map/all_to_all | solution.py:213
  208.9 1.9 copy-start
  210.8 83.9 %all-to-all-start.1 = ((bf16[32,6,72,128]{3,2,1,0:T(8,128)(2,1)}), bf16[32,6,72,128]{3,2,1,0:T(8,128)(2,1)}, u32[]{:S(2)}, u32[]{:S(2)}) async-start(bf16[32,6,72,128]{3,2,1,0:T(8,128)(2,1)} %bitcast.77), calls=%async_computation.1 | async-start | bytes 7077888 | tf_op jit(solution)/shard_map/all_to_all | solution.py:213
  294.7 4.3 %copy-start.6 = (s32[8,12]{1,0:T(8,128)S(1)}, s32[8,12]{1,0:T(8,128)}, u32[]{:S(2)}) copy-start(s32[8,12]{1,0:T(8,128)} %param.9) | copy-start | bytes 1156
  294.7 4.4 %copy-start.5 = (s32[4,24]{1,0:T(4,128)S(1)}, s32[4,24]{1,0:T(4,128)}, u32[]{:S(2)}) copy-start(s32[4,24]{1,0:T(4,128)} %copy-done.4) | copy-start | bytes 1156
  294.7 4.4 %copy-start.10 = (s32[4,24]{1,0:T(4,128)S(1)}, s32[4,24]{1,0:T(4,128)}, u32[]{:S(2)}) copy-start(s32[4,24]{1,0:T(4,128)} %copy-done.9) | copy-start | bytes 1156
  294.7 5.9 %copy-start.8 = (s32[8,12]{1,0:T(8,128)S(1)}, s32[8,12]{1,0:T(8,128)}, u32[]{:S(2)}) copy-start(s32[8,12]{1,0:T(8,128)} %param.8) | copy-start | bytes 1156
  294.7 84.0 %all-to-all-start = ((bf16[32,6,72,128]{3,2,1,0:T(8,128)(2,1)}), bf16[32,6,72,128]{3,2,1,0:T(8,128)(2,1)}, u32[]{:S(2)}, u32[]{:S(2)}) async-start(bf16[32,6,72,128]{3,2,1,0:T(8,128)(2,1)} %bitcast.76), calls=%async_computation | async-start | bytes 7077888 | tf_op jit(solution)/shard_map/all_to_all | solution.py:213
  316.6 2.5 copy-start.3
  319.1 9.0 %copy-start.1 = (bf16[32,6,72,128]{3,2,1,0:T(8,128)(2,1)S(1)}, bf16[32,6,72,128]{3,2,1,0:T(8,128)(2,1)}, u32[]{:S(2)}) copy-start(bf16[32,6,72,128]{3,2,1,0:T(8,128)(2,1)} %copy-done) | copy-start | bytes 10616836

commit v2 on v1

v2 whole, which is shorter than its diff:
```python
import functools

import jax
import jax.numpy as jnp
from jax import lax
from jax.experimental import pallas as pl
from jax.experimental.pallas import tpu as pltpu
from jax.sharding import PartitionSpec as P

DEPTHS = 512
TILE_DEV = 1
TILE_BLK = 20
CAP = 6
LANES = 128


floor_value = 0.25
band_mhz = 288.0
depth_step = 32.0


def faraday_table(parts, part_channels, depths):
    channels = parts * part_channels
    chan_index = jnp.arange(channels, dtype=jnp.float32)
    frequency = 800.0 + (chan_index + 0.5) * (band_mhz / channels)
    lambda_sq = 299.792458 / frequency * (299.792458 / frequency)
    shifted = lambda_sq - jnp.mean(lambda_sq)
    depth_grid = (jnp.arange(depths, dtype=jnp.float32) - depths // 2) * depth_step
    phase_angle = 2.0 * depth_grid[:, None] * shifted[None, :]
    cosine = jnp.cos(phase_angle).reshape(depths, parts, part_channels)
    sine_part = jnp.sin(phase_angle).reshape(depths, parts, part_channels)
    real_rows = jnp.stack([cosine, sine_part], axis=2).reshape(depths, 2 * channels)
    imag_rows = jnp.stack([-sine_part, cosine], axis=2).reshape(depths, 2 * channels)
    table = jnp.concatenate([real_rows, imag_rows], axis=0) / jnp.sqrt(jnp.float32(channels))
    return table.astype(jnp.bfloat16)


def send_body(
    first_tile,
    width,
    obs,
    pattern,
    tile_s,
    corr_ref,
    out,
    mix,
    obs_buf,
    pat_buf,
    pat_wide,
    out_buf,
    count,
    in_sem,
    pat_sem,
    out_sem,
):
    blk_beam, chan_dev, stokes_in, beam_dev, pixels = obs.shape
    beam_count, chan_count = out.shape[:2]
    beams = pattern.shape[1]
    tiles = pixels // chan_count // LANES
    depth = obs_buf.shape[0]
    lanes = width * LANES
    rows = 2 * chan_dev
    beam_row = lax.axis_index("beam")

    def obs_copies(k, slot):
        return [
            pltpu.make_async_copy(
                obs.at[k, :, :, :, pl.ds((part * tiles + first_tile + w) * LANES, LANES)],
                obs_buf.at[slot, part * width + w],
                in_sem.at[slot, part * width + w],
            )
            for part in range(chan_count)
            for w in range(width)
        ]

    def out_copy(slot, d, owner, rank):
        return pltpu.make_async_copy(
            out_buf.at[slot, d], out.at[owner, :, rank], out_sem.at[slot, d]
        )

    pat_copies = [
        pltpu.make_async_copy(
            pattern.at[:, :, pl.ds((part * tiles + first_tile) * LANES, lanes)],
            pat_buf.at[part],
            pat_sem.at[part],
        )
        for part in range(chan_count)
    ]
    for copy in obs_copies(0, 0) + pat_copies:
        copy.start()
    for k in range(1, depth):
        for copy in obs_copies(k, k):
            copy.start()

    identity = (
        lax.broadcasted_iota(jnp.int32, (chan_dev, chan_dev), 0)
        == lax.broadcasted_iota(jnp.int32, (chan_dev, chan_dev), 1)
    ).astype(jnp.float32)
    columns = lax.dot_general(
        identity,
        corr_ref[...],
        (((1,), (1,)), ((), ())),
        precision=lax.Precision.HIGHEST,
        preferred_element_type=jnp.float32,
    )
    inner = stokes_in * beam_dev
    wide = (chan_dev, chan_dev * inner)
    offset = lax.broadcasted_iota(jnp.int32, wide, 1) - inner * lax.broadcasted_iota(jnp.int32, wide, 0)
    high, low = [], []
    for d in range(beam_dev):
        for s in range(2):
            block = jnp.zeros(wide, jnp.float32)
            for t in range(stokes_in):
                column = (d * stokes_in + t) * 2 + s
                block = jnp.where(offset == t * beam_dev + d, columns[:, column : column + 1], block)
            top = block.astype(jnp.bfloat16).astype(jnp.float32)
            high.append(top)
            low.append(block - top)
    mix[...] = jnp.concatenate(high + low, axis=0).astype(jnp.bfloat16)

    for owner in range(beam_count):
        count[owner] = 0
    for copy in pat_copies:
        copy.wait()
    for part in range(chan_count):
        for w in range(width):
            for k in range(blk_beam):
                pat_wide[part * width + w, k * beams : (k + 1) * beams] = pat_buf[
                    part, k, :, w * LANES : (w + 1) * LANES
                ].astype(jnp.float32)

    def block(k, carry):
        slot = lax.rem(k, depth)
        side = lax.rem(k, 2)
        for copy in obs_copies(k, slot):
            copy.wait()

        @pl.when(k >= 2)
        def _():
            for d in range(beam_dev):
                out_copy(side, d, 0, 0).wait()

        for part in range(chan_count):
            for w in range(width):
                observed = obs_buf[slot, part * width + w].reshape(-1, LANES)
                mixed = jnp.dot(mix[...], observed, preferred_element_type=jnp.float32)
                corrected = mixed[: beam_dev * rows] + mixed[beam_dev * rows :]
                for d in range(beam_dev):
                    weight = pat_wide[
                        part * width + w, pl.ds(k * beams + beam_row * beam_dev + d, 1)
                    ]
                    out_buf[side, d, part, :, w * LANES : (w + 1) * LANES] = (
                        corrected[d * rows : (d + 1) * rows] * weight
                    ).astype(jnp.bfloat16)
        for d in range(beam_dev):
            owner = tile_s[beam_row * beam_dev + d, k] // TILE_DEV
            rank = count[owner]
            count[owner] = rank + 1
            out_copy(side, d, owner, rank).start()

        @pl.when(k + depth < blk_beam)
        def _():
            for copy in obs_copies(k + depth, slot):
                copy.start()

        return carry

    lax.fori_loop(0, blk_beam, block, 0)
    for side in range(2):
        for d in range(beam_dev):
            out_copy(side, d, 0, 0).wait()


def send_chunk(obs_t, pattern_t, block_tile, corr_t, beam_count, chan_count, first_tile, width):
    blk_beam, chan_dev, stokes_in, beam_dev, pixels = obs_t.shape
    rows = chan_dev * 2
    lanes = width * LANES
    beams = pattern_t.shape[1]
    depth = 4
    anywhere = pl.BlockSpec(memory_space=pltpu.HBM)
    return pl.pallas_call(
        functools.partial(send_body, first_tile, width),
        out_shape=jax.ShapeDtypeStruct((beam_count, chan_count, CAP, rows, lanes), jnp.bfloat16),
        in_specs=[
            anywhere,
            anywhere,
            pl.BlockSpec(memory_space=pltpu.SMEM),
            pl.BlockSpec(memory_space=pltpu.VMEM),
        ],
        out_specs=anywhere,
        scratch_shapes=[
            pltpu.VMEM((2 * beam_dev * rows, chan_dev * stokes_in * beam_dev), jnp.bfloat16),
            pltpu.VMEM(
                (depth, chan_count * width, chan_dev, stokes_in, beam_dev, LANES), jnp.bfloat16
            ),
            pltpu.VMEM((chan_count, blk_beam, beams, lanes), jnp.bfloat16),
            pltpu.VMEM((chan_count * width, blk_beam * beams, LANES), jnp.float32),
            pltpu.VMEM((2, beam_dev, chan_count, rows, lanes), jnp.bfloat16),
            pltpu.SMEM((beam_count,), jnp.int32),
            pltpu.SemaphoreType.DMA((depth, chan_count * width)),
            pltpu.SemaphoreType.DMA((chan_count,)),
            pltpu.SemaphoreType.DMA((2, beam_dev)),
        ],
        compiler_params=pltpu.CompilerParams(vmem_limit_bytes=48 << 20),
        name=f"send_tile_{first_tile}",
    )(obs_t, pattern_t, block_tile, corr_t)


def sky_body(pair, first_tile, order_s, start_s, recv, inverse_ref, table_ref, *refs):
    out_ref, blocks, total, sem = refs[-4:]
    step = pl.program_id(0)
    parts, rows, lanes = blocks.shape[1:]
    entries = blocks.shape[0]
    slots = pair * pl.num_programs(0)

    def entry_copy(i, source, rank):
        return pltpu.make_async_copy(recv.at[source, :, rank], blocks.at[i], sem.at[i])

    @pl.when(step == 0)
    def _():
        def begin(i, carry):
            entry_copy(i, order_s[0, i], order_s[1, i]).start()
            return carry

        lax.fori_loop(0, start_s[slots], begin, 0)

    for side in range(pair):
        slot = step * pair + side
        columns = slice(side * lanes, (side + 1) * lanes)
        total[:, columns] = jnp.zeros_like(total[:, columns])

        def add(i, carry):
            entry_copy(i, 0, 0).wait()
            for part in range(parts):
                total[part * rows : (part + 1) * rows, columns] += blocks[i, part].astype(jnp.float32)
            return carry

        lax.fori_loop(start_s[slot], start_s[slot + 1], add, 0)
    tiles = lanes // LANES
    sky = jnp.concatenate(
        [
            total[:, tile * LANES : (tile + 1) * LANES]
            * inverse_ref[first_tile + tile % tiles, pl.ds(step * pair + tile // tiles, 1)]
            for tile in range(pair * tiles)
        ],
        axis=1,
    ).astype(jnp.bfloat16)
    spectrum = jnp.dot(table_ref[...], sky, preferred_element_type=jnp.float32)
    for side in range(pair):
        out_ref[side] = spectrum[:, side * lanes : (side + 1) * lanes].astype(out_ref.dtype)


def sky_chunk(recv, inverse, table, order, start, first_tile, width, tiles, earlier):
    pair = 2
    slots = inverse.shape[1]
    lanes = width * LANES
    beam_count, parts, capacity, rows = recv.shape[:4]
    anywhere = pl.BlockSpec(memory_space=pltpu.HBM)
    whole = lambda a: pl.BlockSpec(a.shape, lambda l, *s: (0,) * a.ndim)
    in_specs = [anywhere, whole(inverse), whole(table)]
    args = [order, start, recv, inverse, table]
    aliases = {}
    if earlier is not None:
        in_specs.append(anywhere)
        aliases = {len(args): 0}
        args.append(earlier)
    return pl.pallas_call(
        functools.partial(sky_body, pair, first_tile),
        out_shape=jax.ShapeDtypeStruct((slots, table.shape[0], tiles * LANES), jnp.bfloat16),
        grid_spec=pltpu.PrefetchScalarGridSpec(
            num_scalar_prefetch=2,
            grid=(slots // pair,),
            in_specs=in_specs,
            out_specs=pl.BlockSpec(
                (pl.Element(pair), pl.Element(table.shape[0]), pl.Element(lanes)),
                lambda l, *s: (l * pair, 0, first_tile * LANES),
            ),
            scratch_shapes=[
                pltpu.VMEM((beam_count * capacity, parts, rows, lanes), jnp.bfloat16),
                pltpu.VMEM((table.shape[1], pair * lanes), jnp.float32),
                pltpu.SemaphoreType.DMA((beam_count * capacity,)),
            ],
        ),
        input_output_aliases=aliases,
        compiler_params=pltpu.CompilerParams(vmem_limit_bytes=48 << 20),
        name=f"sky_tile_{first_tile}",
    )(*args)


def received_order(block_tile, block_offset, beam_row, beam_count, beam_dev, blk_beam):
    local_slots = TILE_DEV * TILE_BLK

    def by_block(a):
        return jnp.swapaxes(a.reshape(beam_count, beam_dev, blk_beam), 1, 2).reshape(beam_count, -1)

    tile = by_block(block_tile)
    slot_of = tile % TILE_DEV * TILE_BLK + by_block(block_offset)
    mine = tile // TILE_DEV == beam_row
    position = jnp.arange(beam_dev * blk_beam, dtype=jnp.int32)
    earlier = position[None, :] < position[:, None]
    rank_in = jnp.sum((mine[:, None, :] & earlier[None]).astype(jnp.int32), axis=2)
    ranks = jnp.arange(CAP, dtype=jnp.int32)
    hit = mine[:, :, None] & (rank_in[:, :, None] == ranks[None, None, :])
    entry_slot = jnp.min(jnp.where(hit, slot_of[:, :, None], local_slots), axis=1).reshape(-1)
    index = jnp.arange(beam_count * CAP, dtype=jnp.int32)
    before = (entry_slot[None, :] < entry_slot[:, None]) | (
        (entry_slot[None, :] == entry_slot[:, None]) & (index[None, :] < index[:, None])
    )
    place = jnp.sum(before.astype(jnp.int32), axis=1)
    order = jnp.sum(jnp.where(place[None, :] == index[:, None], index[None, :], 0), axis=1)
    slot_index = jnp.arange(local_slots + 1, dtype=jnp.int32)
    start = jnp.sum((entry_slot[None, :] < slot_index[:, None]).astype(jnp.int32), axis=1)
    return jnp.stack([order // CAP, order % CAP]), start


def pixel_chunks(tiles):
    if tiles < 4:
        return [(tile, 1) for tile in range(tiles)]
    return [(0, 1), (1, tiles - 2), (tiles - 1, 1)]


def shards(observed, beam_pattern, correction, block_tile, block_offset):
    beam_count = lax.axis_size("beam")
    chan_count = lax.axis_size("chan")
    beam_row = lax.axis_index("beam")
    chan_part = lax.axis_index("chan")
    beam_dev, blk_beam, chan_dev, stokes_in, pixels = observed.shape
    pixel_share = pixels // chan_count
    tiles = pixel_share // LANES
    local_slots = TILE_DEV * TILE_BLK

    obs_t = jnp.transpose(observed, (1, 2, 3, 0, 4))
    pattern_t = jnp.transpose(beam_pattern, (1, 0, 2))
    corr_t = jnp.transpose(correction, (0, 3, 2, 1)).reshape(-1, chan_dev)

    order, start = received_order(
        block_tile, block_offset, beam_row, beam_count, beam_dev, blk_beam
    )
    global_slot = (block_tile * TILE_BLK + block_offset).reshape(-1)
    slot_range = beam_row * local_slots + jnp.arange(local_slots, dtype=jnp.int32)
    cover = (global_slot[None, :] == slot_range[:, None]).astype(jnp.float32)
    share = lax.dynamic_slice_in_dim(beam_pattern, chan_part * pixel_share, pixel_share, 2)
    share = share.astype(jnp.float32).reshape(-1, pixel_share)
    weight_sum = jnp.dot(cover, share * share, precision=lax.Precision.HIGHEST)
    inverse = 1.0 / jnp.maximum(weight_sum, floor_value)
    inverse = jnp.swapaxes(inverse.reshape(local_slots, tiles, LANES), 0, 1)
    table = faraday_table(chan_count, chan_dev, DEPTHS)

    spectrum = None
    for first_tile, width in pixel_chunks(tiles):
        sent = send_chunk(
            obs_t, pattern_t, block_tile, corr_t, beam_count, chan_count, first_tile, width
        )
        received = lax.all_to_all(
            sent.reshape((beam_count * chan_count,) + sent.shape[2:]),
            ("beam", "chan"),
            split_axis=0,
            concat_axis=0,
            tiled=True,
        ).reshape(sent.shape)
        spectrum = sky_chunk(
            received,
            inverse,
            table,
            order,
            start,
            first_tile,
            width,
            tiles,
            spectrum,
        )
    return spectrum.reshape(TILE_DEV, TILE_BLK, 2, DEPTHS, pixel_share)


def solution(mesh):
    placed = (P("beam", None, "chan", None, None), P(), P("beam", "chan", None, None), P(), P())
    return jax.shard_map(
        shards,
        mesh=mesh,
        in_specs=placed,
        out_specs=P("beam", None, None, None, "chan"),
        check_vma=False,
    )
```

time: 394 us -> 358 us (0.909)
  Pallas kernels: 125 us -> 68 us
  waiting for transfers between devices: 206 us -> 250 us
  local copies, waits for them, and re-layouts: 28.7 us -> 16.5 us
  starting transfers between devices: 19.7 us -> 15.1 us
    pallas_call x8 -> x6, Pallas kernels: 125 us -> 68 us  [the longest x3 35.2 us: sky_chunk(): pl.pallas_call(functools.partial(sky_body, pair, first_tile), out_shape=j...]
    all_to_all x4 -> x3, waiting for transfers between devices: 206 us -> 250 us  [shards(): lax.all_to_all(sent.reshape((beam_count * chan_count,) + sent.shape[2:]),...]
    mul x5 -> x0, local copies, waits for them, and re-layouts: 9.92 us -> none  [shards(): correction[:, :, :, None, :, None] * same_chan[None, :, None, :, None, None]]
    all_to_all x4 -> x3, starting transfers between devices: 19.7 us -> 15.1 us  [shards(): lax.all_to_all(sent.reshape((beam_count * chan_count,) + sent.shape[2:]),...]
    unnamed x25 -> x18, local copies, waits for them, and re-layouts: 3.78 us -> 8.23 us
  transfers between devices with their start and end apart: 4 -> 3, of which waited for: 4 -> 3; matrix products, arithmetic and copies ran while one was open for 5% -> 4% of each run, Pallas kernels for 24% -> 14%
where the time goes in v2:
time: 358 us
  waiting for transfers between devices  250 us (70%)
  Pallas kernels  68 us (19%)
  local copies, waits for them, and re-layouts  16.5 us (5%)
  starting transfers between devices  15.1 us (4%)
  other arithmetic  6.75 us (2%)
    all_to_all x3, waiting for transfers between devices, shards(): lax.all_to_all(sent.reshape((beam_count * chan_count,) + sent.shape[2:]),...  250 us
    pallas_call x3, Pallas kernels, sky_chunk(): pl.pallas_call(functools.partial(sky_body, pair, first_tile), out_shape=j...  35.2 us
    pallas_call x3, Pallas kernels, send_chunk(): pl.pallas_call(functools.partial(send_body, first_tile, width), out_shape...  32.8 us
    all_to_all x3, starting transfers between devices, shards(): lax.all_to_all(sent.reshape((beam_count * chan_count,) + sent.shape[2:]),...  15.1 us
    unnamed x18, local copies, waits for them, and re-layouts  8.23 us
  transfers between devices with their start and end apart: 3, of which 3 were waited for; matrix products, arithmetic and copies ran while one was open for 4% of the time, Pallas kernels for 14%

profile of v2, /device:TPU:0, one launch (start us, length us, event | category | flops | bytes accessed | tf_op | source)
XLA Modules:
  0.0 357.6 jit_solution(10304931587145218588)
XLA Ops:
  0.0 0.7 reshape.200.corr_ref
  0.7 1.1 copy-done.3
  1.8 0.7 copy-done.6
  2.5 9.2 %send_tile_0.1 = bf16[4,8,6,72,128]{4,3,2,1,0:T(8,128)(2,1)S(1)} custom-call(bf16[12,36,3,2,4096]{4,3,2,1,0:T(2,128)(2,1)} %bitcast.40, bf16[12,8,4096]{2,1,0:T(8,128)(2,1)S(1)} %bitcast.34, s32[8,12]{1,0:T(8,128)S(1)} %copy-done.6, f32[12,36]{1,0:T(8,128)S(1)} %reshape.200.corr_ref), custom_call_target="tpu_custom_call" | custom-call | tf_op jit(solution)/shard_map/send_tile_0/pallas_call | solution.py:181
  11.7 0.0 copy-start.2
  11.7 1.7 copy-done.2
  13.5 7.3 %all-to-all-start.2 = ((bf16[32,6,72,128]{3,2,1,0:T(8,128)(2,1)}), bf16[32,6,72,128]{3,2,1,0:T(8,128)(2,1)S(1)}, u32[]{:S(2)}, u32[]{:S(2)}) async-start(bf16[32,6,72,128]{3,2,1,0:T(8,128)(2,1)} %bitcast.33), calls=%async_computation.2 | async-start | bytes 7077888 | tf_op jit(solution)/shard_map/all_to_all | solution.py:354
  20.8 0.0 copy-done.7
  20.8 0.0 copy-start.4
  20.8 1.1 copy-done.4
  21.9 13.6 %send_tile_1.1 = bf16[4,8,6,72,256]{4,3,2,1,0:T(8,128)(2,1)} custom-call(bf16[12,36,3,2,4096]{4,3,2,1,0:T(2,128)(2,1)} %bitcast.41, bf16[12,8,4096]{2,1,0:T(8,128)(2,1)S(1)} %bitcast.35, s32[8,12]{1,0:T(8,128)S(1)} %copy-done.7, f32[12,36]{1,0:T(8,128)S(1)} %reshape.200.corr_ref), custom_call_target="tpu_custom_call" | custom-call | tf_op jit(solution)/shard_map/send_tile_1/pallas_call | solution.py:181
  35.5 65.1 %all-to-all-done.2 = bf16[32,6,72,128]{3,2,1,0:T(8,128)(2,1)S(1)} async-done(((bf16[32,6,72,128]{3,2,1,0:T(8,128)(2,1)}), bf16[32,6,72,128]{3,2,1,0:T(8,128)(2,1)S(1)}, u32[]{:S(2)}, u32[]{:S(2)}) %all-to-all-start.2) | async-done | bytes 3538976 | tf_op jit(solution)/shard_map/all_to_all | solution.py:354
  100.6 1.7 copy-done
  102.3 4.1 %all-to-all-start.1 = ((bf16[32,6,72,256]{3,2,1,0:T(8,128)(2,1)}), bf16[32,6,72,256]{3,2,1,0:T(8,128)(2,1)}, u32[]{:S(2)}, u32[]{:S(2)}) async-start(bf16[32,6,72,256]{3,2,1,0:T(8,128)(2,1)} %bitcast.43), calls=%async_computation.1 | async-start | bytes 14155776 | tf_op jit(solution)/shard_map/all_to_all | solution.py:354
  106.5 0.0 copy-start.5
  106.5 1.1 copy-done.5
  107.6 10.0 %send_tile_3.1 = bf16[4,8,6,72,128]{4,3,2,1,0:T(8,128)(2,1)} custom-call(bf16[12,36,3,2,4096]{4,3,2,1,0:T(2,128)(2,1)} %bitcast.42, bf16[12,8,4096]{2,1,0:T(8,128)(2,1)S(1)} %bitcast.36, s32[8,12]{1,0:T(8,128)S(1)} %copy-done.7, f32[12,36]{1,0:T(8,128)S(1)} %reshape.200.corr_ref), custom_call_target="tpu_custom_call" | custom-call | tf_op jit(solution)/shard_map/send_tile_3/pallas_call | solution.py:181
  117.6 146.2 %all-to-all-done.1 = bf16[32,6,72,256]{3,2,1,0:T(8,128)(2,1)} async-done(((bf16[32,6,72,256]{3,2,1,0:T(8,128)(2,1)}), bf16[32,6,72,256]{3,2,1,0:T(8,128)(2,1)}, u32[]{:S(2)}, u32[]{:S(2)}) %all-to-all-start.1) | async-done | bytes 7077920 | tf_op jit(solution)/shard_map/all_to_all | solution.py:354
  263.8 3.7 %all-to-all-start = ((bf16[32,6,72,128]{3,2,1,0:T(8,128)(2,1)}), bf16[32,6,72,128]{3,2,1,0:T(8,128)(2,1)}, u32[]{:S(2)}, u32[]{:S(2)}) async-start(bf16[32,6,72,128]{3,2,1,0:T(8,128)(2,1)} %bitcast.10), calls=%async_computation | async-start | bytes 7077888 | tf_op jit(solution)/shard_map/all_to_all | solution.py:354
  267.5 0.1 copy.18
  267.7 0.1 eq.79
  267.8 0.0 copy-done.8
  267.8 0.1 copy.19
  267.9 0.1 copy.20
  268.0 0.2 convert_reduce_fusion
  268.1 0.2 select_reduce_fusion.1
  268.3 0.1 copy.21
  268.4 0.1 lt.78
  268.5 0.6 fusion.7
  269.8 2.4 multiply_sine_fusion
  272.2 0.3 pad_maximum_fusion
  272.5 1.1 reshape.204
  273.6 1.7 copy.24
  275.3 1.2 reshape.205
  276.5 2.7 copy.25
  279.2 0.9 convert_multiply_fusion
  280.1 0.1 copy.22
  280.3 0.1 eq.86
  280.4 0.2 fusion.1
  280.7 0.2 convert_reduce_fusion.2
  280.9 0.1 select_reduce_fusion
  281.0 0.1 convert_reduce_fusion.1.start_s
  281.1 1.7 fusion.table_ref
  282.9 0.7 copy-done.1
  283.5 10.0 %sky_tile_0.1.refs_0_ = bf16[20,1024,512]{2,1,0:T(8,128)(2,1)} custom-call(s32[2,24]{1,0:T(2,128)S(1)} %pad_add_fusion.order_s, s32[21]{0:T(128)S(1)} %convert_reduce_fusion.1.start_s, bf16[4,8,6,72,128]{4,3,2,1,0:T(8,128)(2,1)S(1)} %bitcast.32, f32[4,20,128]{2,1,0:T(8,128)S(1)} %bitcast.37, bf16[1024,576]{1,0:T(8,128)(2,1)S(1)} %fusion.table_ref), custom_call_target="tpu_custom_call" | custom-call | tf_op jit(solution)/shard_map/sky_tile_0/pallas_call | solution.py:267
  293.6 15.0 %sky_tile_1.1.refs_0_ = bf16[20,1024,512]{2,1,0:T(8,128)(2,1)} custom-call(s32[2,24]{1,0:T(2,128)S(1)} %pad_add_fusion.order_s, s32[21]{0:T(128)S(1)} %convert_reduce_fusion.1.start_s, bf16[4,8,6,72,256]{4,3,2,1,0:T(8,128)(2,1)} %bitcast.14.recv, f32[4,20,128]{2,1,0:T(8,128)S(1)} %bitcast.38, ...), custom_call_target="tpu_custom_call", output_to_operand_aliasing={{}: (5, {})} | custom-call | tf_op jit(solution)/shard_map/sky_tile_1/pallas_call | solution.py:267
  308.6 38.9 %all-to-all-done = bf16[32,6,72,128]{3,2,1,0:T(8,128)(2,1)} async-done(((bf16[32,6,72,128]{3,2,1,0:T(8,128)(2,1)}), bf16[32,6,72,128]{3,2,1,0:T(8,128)(2,1)}, u32[]{:S(2)}, u32[]{:S(2)}) %all-to-all-start) | async-done | bytes 3538976 | tf_op jit(solution)/shard_map/all_to_all | solution.py:354
  347.4 10.1 %sky_tile_3.1 = bf16[20,1024,512]{2,1,0:T(8,128)(2,1)} custom-call(s32[2,24]{1,0:T(2,128)S(1)} %pad_add_fusion.order_s, s32[21]{0:T(128)S(1)} %convert_reduce_fusion.1.start_s, bf16[4,8,6,72,128]{4,3,2,1,0:T(8,128)(2,1)} %bitcast.11.recv, f32[4,20,128]{2,1,0:T(8,128)S(1)} %bitcast.39, ...), custom_call_target="tpu_custom_call", output_to_operand_aliasing={{}: (5, {})} | custom-call | tf_op jit(solution)/shard_map/sky_tile_3/pallas_call | solution.py:267
  (18 shorter events, 0.1 us)
Async XLA Ops:
  0.7 1.1 copy-start.3
  1.8 0.7 copy-start.6
  11.7 1.8 copy-start.2
  13.5 7.3 %copy-start.7 = (s32[8,12]{1,0:T(8,128)S(1)}, s32[8,12]{1,0:T(8,128)}, u32[]{:S(2)}) copy-start(s32[8,12]{1,0:T(8,128)} %tile_s.5) | copy-start | bytes 1156
  13.5 87.1 %all-to-all-start.2 = ((bf16[32,6,72,128]{3,2,1,0:T(8,128)(2,1)}), bf16[32,6,72,128]{3,2,1,0:T(8,128)(2,1)S(1)}, u32[]{:S(2)}, u32[]{:S(2)}) async-start(bf16[32,6,72,128]{3,2,1,0:T(8,128)(2,1)} %bitcast.33), calls=%async_computation.2 | async-start | bytes 7077888 | tf_op jit(solution)/shard_map/all_to_all | solution.py:354
  20.8 1.1 copy-start.4
  100.6 1.7 copy-start
  102.3 161.5 %all-to-all-start.1 = ((bf16[32,6,72,256]{3,2,1,0:T(8,128)(2,1)}), bf16[32,6,72,256]{3,2,1,0:T(8,128)(2,1)}, u32[]{:S(2)}, u32[]{:S(2)}) async-start(bf16[32,6,72,256]{3,2,1,0:T(8,128)(2,1)} %bitcast.43), calls=%async_computation.1 | async-start | bytes 14155776 | tf_op jit(solution)/shard_map/all_to_all | solution.py:354
  106.5 1.1 copy-start.5
  263.8 3.9 %copy-start.8 = (s32[8,12]{1,0:T(8,128)S(1)}, s32[8,12]{1,0:T(8,128)}, u32[]{:S(2)}) copy-start(s32[8,12]{1,0:T(8,128)} %param.9) | copy-start | bytes 1156
  263.8 83.6 %all-to-all-start = ((bf16[32,6,72,128]{3,2,1,0:T(8,128)(2,1)}), bf16[32,6,72,128]{3,2,1,0:T(8,128)(2,1)}, u32[]{:S(2)}, u32[]{:S(2)}) async-start(bf16[32,6,72,128]{3,2,1,0:T(8,128)(2,1)} %bitcast.10), calls=%async_computation | async-start | bytes 7077888 | tf_op jit(solution)/shard_map/all_to_all | solution.py:354
  281.1 2.4 copy-start.1

commit v3 on v2

--- a/solution.py
+++ b/solution.py
@@ -35,14 +35,20 @@
     return table.astype(jnp.bfloat16)
 
 
+def in_hbm(array):
+    return pltpu.with_memory_space_constraint(array, pltpu.HBM)
+
+
 def send_body(
     first_tile,
     width,
     obs,
     pattern,
+    block_tile,
+    correction,
+    out,
     tile_s,
     corr_ref,
-    out,
     mix,
     obs_buf,
     pat_buf,
@@ -52,6 +58,8 @@
     in_sem,
     pat_sem,
     out_sem,
+    tile_sem,
+    corr_sem,
 ):
     blk_beam, chan_dev, stokes_in, beam_dev, pixels = obs.shape
     beam_count, chan_count = out.shape[:2]
@@ -86,7 +94,10 @@
         )
         for part in range(chan_count)
     ]
-    for copy in obs_copies(0, 0) + pat_copies:
+    tile_copy = pltpu.make_async_copy(block_tile, tile_s, tile_sem)
+    corr_copy = pltpu.make_async_copy(correction, corr_ref, corr_sem)
+    corr_copy.start()
+    for copy in obs_copies(0, 0) + pat_copies + [tile_copy]:
         copy.start()
     for k in range(1, depth):
         for copy in obs_copies(k, k):
@@ -96,13 +107,20 @@
         lax.broadcasted_iota(jnp.int32, (chan_dev, chan_dev), 0)
         == lax.broadcasted_iota(jnp.int32, (chan_dev, chan_dev), 1)
     ).astype(jnp.float32)
-    columns = lax.dot_general(
-        identity,
-        corr_ref[...],
-        (((1,), (1,)), ((), ())),
-        precision=lax.Precision.HIGHEST,
-        preferred_element_type=jnp.float32,
-    )
+    corr_copy.wait()
+    columns = [
+        [
+            lax.dot_general(
+                identity,
+                corr_ref[d, t],
+                (((1,), (1,)), ((), ())),
+                precision=lax.Precision.HIGHEST,
+                preferred_element_type=jnp.float32,
+            )
+            for t in range(stokes_in)
+        ]
+        for d in range(beam_dev)
+    ]
     inner = stokes_in * beam_dev
     wide = (chan_dev, chan_dev * inner)
     offset = lax.broadcasted_iota(jnp.int32, wide, 1) - inner * lax.broadcasted_iota(jnp.int32, wide, 0)
@@ -111,8 +129,7 @@
         for s in range(2):
             block = jnp.zeros(wide, jnp.float32)
             for t in range(stokes_in):
-                column = (d * stokes_in + t) * 2 + s
-                block = jnp.where(offset == t * beam_dev + d, columns[:, column : column + 1], block)
+                block = jnp.where(offset == t * beam_dev + d, columns[d][t][:, s : s + 1], block)
             top = block.astype(jnp.bfloat16).astype(jnp.float32)
             high.append(top)
             low.append(block - top)
@@ -120,7 +137,7 @@
 
     for owner in range(beam_count):
         count[owner] = 0
-    for copy in pat_copies:
+    for copy in pat_copies + [tile_copy]:
         copy.wait()
     for part in range(chan_count):
         for w in range(width):
@@ -180,15 +197,17 @@
     anywhere = pl.BlockSpec(memory_space=pltpu.HBM)
     return pl.pallas_call(
         functools.partial(send_body, first_tile, width),
-        out_shape=jax.ShapeDtypeStruct((beam_count, chan_count, CAP, rows, lanes), jnp.bfloat16),
+        out_shape=pltpu.HBM((beam_count, chan_count, CAP, rows, lanes), jnp.bfloat16),
         in_specs=[
             anywhere,
             anywhere,
-            pl.BlockSpec(memory_space=pltpu.SMEM),
-            pl.BlockSpec(memory_space=pltpu.VMEM),
+            anywhere,
+            anywhere,
         ],
         out_specs=anywhere,
         scratch_shapes=[
+            pltpu.SMEM(block_tile.shape, jnp.int32),
+            pltpu.VMEM(corr_t.shape, jnp.float32),
             pltpu.VMEM((2 * beam_dev * rows, chan_dev * stokes_in * beam_dev), jnp.bfloat16),
             pltpu.VMEM(
                 (depth, chan_count * width, chan_dev, stokes_in, beam_dev, LANES), jnp.bfloat16
@@ -200,10 +219,12 @@
             pltpu.SemaphoreType.DMA((depth, chan_count * width)),
             pltpu.SemaphoreType.DMA((chan_count,)),
             pltpu.SemaphoreType.DMA((2, beam_dev)),
+            pltpu.SemaphoreType.DMA(()),
+            pltpu.SemaphoreType.DMA(()),
         ],
-        compiler_params=pltpu.CompilerParams(vmem_limit_bytes=48 << 20),
+        compiler_params=pltpu.CompilerParams(vmem_limit_bytes=61 << 20),
         name=f"send_tile_{first_tile}",
-    )(obs_t, pattern_t, block_tile, corr_t)
+    )(obs_t, in_hbm(pattern_t), in_hbm(block_tile), in_hbm(corr_t))
 
 
 def sky_body(pair, first_tile, order_s, start_s, recv, inverse_ref, table_ref, *refs):
@@ -251,14 +272,14 @@
 
 
 def sky_chunk(recv, inverse, table, order, start, first_tile, width, tiles, earlier):
-    pair = 2
+    pair = 4
     slots = inverse.shape[1]
     lanes = width * LANES
     beam_count, parts, capacity, rows = recv.shape[:4]
     anywhere = pl.BlockSpec(memory_space=pltpu.HBM)
     whole = lambda a: pl.BlockSpec(a.shape, lambda l, *s: (0,) * a.ndim)
     in_specs = [anywhere, whole(inverse), whole(table)]
-    args = [order, start, recv, inverse, table]
+    args = [order, start, in_hbm(recv), inverse, table]
     aliases = {}
     if earlier is not None:
         in_specs.append(anywhere)
@@ -331,7 +352,7 @@
 
     obs_t = jnp.transpose(observed, (1, 2, 3, 0, 4))
     pattern_t = jnp.transpose(beam_pattern, (1, 0, 2))
-    corr_t = jnp.transpose(correction, (0, 3, 2, 1)).reshape(-1, chan_dev)
+    corr_t = jnp.transpose(correction, (0, 3, 2, 1))
 
     order, start = received_order(
         block_tile, block_offset, beam_row, beam_count, beam_dev, blk_beam

time: 358 us -> 353 us (0.986)
  local copies, waits for them, and re-layouts: 16.5 us -> 7.58 us
    unnamed x18 -> x4, local copies, waits for them, and re-layouts: 8.23 us -> 0.01 us
where the time goes in v3:
time: 353 us
  waiting for transfers between devices  252 us (71%)
  Pallas kernels  70 us (20%)
  starting transfers between devices  15.3 us (4%)
  local copies, waits for them, and re-layouts  7.58 us (2%)
  other arithmetic  6.6 us (2%)
    all_to_all x3, waiting for transfers between devices, shards(): lax.all_to_all(sent.reshape((beam_count * chan_count,) + sent.shape[2:]),...  252 us
    pallas_call x3, Pallas kernels, send_chunk(): pl.pallas_call(functools.partial(send_body, first_tile, width), out_shape...  35.8 us
    pallas_call x3, Pallas kernels, sky_chunk(): pl.pallas_call(functools.partial(sky_body, pair, first_tile), out_shape=j...  34.2 us
    all_to_all x3, starting transfers between devices, shards(): lax.all_to_all(sent.reshape((beam_count * chan_count,) + sent.shape[2:]),...  15.3 us
  transfers between devices with their start and end apart: 3, of which 3 were waited for; matrix products, arithmetic and copies ran while one was open for 4% of the time, Pallas kernels for 14%

profile of v3, /device:TPU:0, one launch (start us, length us, event | category | flops | bytes accessed | tf_op | source)
XLA Modules:
  0.0 352.8 jit_solution(6626831695671892830)
XLA Ops:
  0.0 10.6 %send_tile_0.1 = bf16[4,8,6,72,128]{4,3,2,1,0:T(8,128)(2,1)} custom-call(bf16[12,36,3,2,4096]{4,3,2,1,0:T(2,128)(2,1)} %bitcast.35, bf16[12,8,4096]{2,1,0:T(8,128)(2,1)} %bitcast.41, s32[8,12]{1,0:T(8,128)} %block_tile.5, f32[2,3,2,36]{3,2,1,0:T(2,128)} %bitcast.44), custom_call_target="tpu_custom_call" | custom-call | tf_op jit(solution)/shard_map/send_tile_0/pallas_call | solution.py:198
  10.6 7.3 %all-to-all-start.2 = ((bf16[32,6,72,128]{3,2,1,0:T(8,128)(2,1)}), bf16[32,6,72,128]{3,2,1,0:T(8,128)(2,1)}, u32[]{:S(2)}, u32[]{:S(2)}) async-start(bf16[32,6,72,128]{3,2,1,0:T(8,128)(2,1)} %bitcast.40), calls=%async_computation.2 | async-start | bytes 7077888 | tf_op jit(solution)/shard_map/all_to_all | solution.py:375
  17.9 14.7 %send_tile_1.1 = bf16[4,8,6,72,256]{4,3,2,1,0:T(8,128)(2,1)} custom-call(bf16[12,36,3,2,4096]{4,3,2,1,0:T(2,128)(2,1)} %bitcast.36, bf16[12,8,4096]{2,1,0:T(8,128)(2,1)} %bitcast.42, s32[8,12]{1,0:T(8,128)} %block_tile.5, f32[2,3,2,36]{3,2,1,0:T(2,128)} %bitcast.45), custom_call_target="tpu_custom_call" | custom-call | tf_op jit(solution)/shard_map/send_tile_1/pallas_call | solution.py:198
  32.7 65.1 %all-to-all-done.2 = bf16[32,6,72,128]{3,2,1,0:T(8,128)(2,1)} async-done(((bf16[32,6,72,128]{3,2,1,0:T(8,128)(2,1)}), bf16[32,6,72,128]{3,2,1,0:T(8,128)(2,1)}, u32[]{:S(2)}, u32[]{:S(2)}) %all-to-all-start.2) | async-done | bytes 3538976 | tf_op jit(solution)/shard_map/all_to_all | solution.py:375
  97.7 4.1 %all-to-all-start.1 = ((bf16[32,6,72,256]{3,2,1,0:T(8,128)(2,1)}), bf16[32,6,72,256]{3,2,1,0:T(8,128)(2,1)}, u32[]{:S(2)}, u32[]{:S(2)}) async-start(bf16[32,6,72,256]{3,2,1,0:T(8,128)(2,1)} %bitcast.38), calls=%async_computation.1 | async-start | bytes 14155776 | tf_op jit(solution)/shard_map/all_to_all | solution.py:375
  101.9 10.5 %send_tile_3.1 = bf16[4,8,6,72,128]{4,3,2,1,0:T(8,128)(2,1)} custom-call(bf16[12,36,3,2,4096]{4,3,2,1,0:T(2,128)(2,1)} %bitcast.37, bf16[12,8,4096]{2,1,0:T(8,128)(2,1)} %bitcast.43, s32[8,12]{1,0:T(8,128)} %block_tile.5, f32[2,3,2,36]{3,2,1,0:T(2,128)} %bitcast.46), custom_call_target="tpu_custom_call" | custom-call | tf_op jit(solution)/shard_map/send_tile_3/pallas_call | solution.py:198
  112.3 146.9 %all-to-all-done.1 = bf16[32,6,72,256]{3,2,1,0:T(8,128)(2,1)} async-done(((bf16[32,6,72,256]{3,2,1,0:T(8,128)(2,1)}), bf16[32,6,72,256]{3,2,1,0:T(8,128)(2,1)}, u32[]{:S(2)}, u32[]{:S(2)}) %all-to-all-start.1) | async-done | bytes 7077920 | tf_op jit(solution)/shard_map/all_to_all | solution.py:375
  259.2 0.0 copy-start
  259.2 0.0 copy-start.1
  259.2 3.9 %all-to-all-start = ((bf16[32,6,72,128]{3,2,1,0:T(8,128)(2,1)}), bf16[32,6,72,128]{3,2,1,0:T(8,128)(2,1)}, u32[]{:S(2)}, u32[]{:S(2)}) async-start(bf16[32,6,72,128]{3,2,1,0:T(8,128)(2,1)} %bitcast.39), calls=%async_computation | async-start | bytes 7077888 | tf_op jit(solution)/shard_map/all_to_all | solution.py:375
  263.1 0.0 copy-done
  263.1 0.1 copy.18
  263.3 0.1 eq.79
  263.4 0.0 copy-done.1
  263.4 0.1 copy.19
  263.5 0.1 copy.20
  263.6 0.2 convert_reduce_fusion
  263.7 0.2 select_reduce_fusion.1
  263.9 0.1 copy.21
  264.0 0.1 lt.78
  264.1 0.6 fusion.7
  265.4 2.4 multiply_sine_fusion
  267.8 0.3 pad_maximum_fusion
  268.1 1.1 reshape.200
  269.2 1.7 copy.24
  270.9 1.2 reshape.201
  272.1 2.7 copy.25
  274.8 0.9 convert_multiply_fusion
  275.7 0.1 copy.22
  275.9 0.1 eq.86
  276.0 0.2 fusion.1
  276.3 0.2 convert_reduce_fusion.2
  276.4 0.1 select_reduce_fusion
  276.6 0.1 convert_reduce_fusion.1.start_s
  276.7 1.6 fusion.table_ref
  278.3 9.7 %sky_tile_0.1.refs_0_ = bf16[20,1024,512]{2,1,0:T(8,128)(2,1)} custom-call(s32[2,24]{1,0:T(2,128)S(1)} %pad_add_fusion.order_s, s32[21]{0:T(128)S(1)} %convert_reduce_fusion.1.start_s, bf16[4,8,6,72,128]{4,3,2,1,0:T(8,128)(2,1)} %bitcast.16.recv, f32[4,20,128]{2,1,0:T(8,128)S(1)} %bitcast.32, bf16[1024,576]{1,0:T(8,128)(2,1)S(1)} %fusion.table_ref), custom_call_target="tpu_custom_call" | custom-call | tf_op jit(solution)/shard_map/sky_tile_0/pallas_call | solution.py:288
  288.0 14.8 %sky_tile_1.1.refs_0_ = bf16[20,1024,512]{2,1,0:T(8,128)(2,1)} custom-call(s32[2,24]{1,0:T(2,128)S(1)} %pad_add_fusion.order_s, s32[21]{0:T(128)S(1)} %convert_reduce_fusion.1.start_s, bf16[4,8,6,72,256]{4,3,2,1,0:T(8,128)(2,1)} %bitcast.14.recv, f32[4,20,128]{2,1,0:T(8,128)S(1)} %bitcast.33, ...), custom_call_target="tpu_custom_call", output_to_operand_aliasing={{}: (5, {})} | custom-call | tf_op jit(solution)/shard_map/sky_tile_1/pallas_call | solution.py:288
  302.8 40.1 %all-to-all-done = bf16[32,6,72,128]{3,2,1,0:T(8,128)(2,1)} async-done(((bf16[32,6,72,128]{3,2,1,0:T(8,128)(2,1)}), bf16[32,6,72,128]{3,2,1,0:T(8,128)(2,1)}, u32[]{:S(2)}, u32[]{:S(2)}) %all-to-all-start) | async-done | bytes 3538976 | tf_op jit(solution)/shard_map/all_to_all | solution.py:375
  342.9 9.7 %sky_tile_3.1 = bf16[20,1024,512]{2,1,0:T(8,128)(2,1)} custom-call(s32[2,24]{1,0:T(2,128)S(1)} %pad_add_fusion.order_s, s32[21]{0:T(128)S(1)} %convert_reduce_fusion.1.start_s, bf16[4,8,6,72,128]{4,3,2,1,0:T(8,128)(2,1)} %bitcast.11.recv, f32[4,20,128]{2,1,0:T(8,128)S(1)} %bitcast.34, ...), custom_call_target="tpu_custom_call", output_to_operand_aliasing={{}: (5, {})} | custom-call | tf_op jit(solution)/shard_map/sky_tile_3/pallas_call | solution.py:288
  (12 shorter events, 0.1 us)
Async XLA Ops:
  10.6 87.1 %all-to-all-start.2 = ((bf16[32,6,72,128]{3,2,1,0:T(8,128)(2,1)}), bf16[32,6,72,128]{3,2,1,0:T(8,128)(2,1)}, u32[]{:S(2)}, u32[]{:S(2)}) async-start(bf16[32,6,72,128]{3,2,1,0:T(8,128)(2,1)} %bitcast.40), calls=%async_computation.2 | async-start | bytes 7077888 | tf_op jit(solution)/shard_map/all_to_all | solution.py:375
  97.7 161.5 %all-to-all-start.1 = ((bf16[32,6,72,256]{3,2,1,0:T(8,128)(2,1)}), bf16[32,6,72,256]{3,2,1,0:T(8,128)(2,1)}, u32[]{:S(2)}, u32[]{:S(2)}) async-start(bf16[32,6,72,256]{3,2,1,0:T(8,128)(2,1)} %bitcast.38), calls=%async_computation.1 | async-start | bytes 14155776 | tf_op jit(solution)/shard_map/all_to_all | solution.py:375
  259.2 3.9 %copy-start = (s32[8,12]{1,0:T(8,128)S(1)}, s32[8,12]{1,0:T(8,128)}, u32[]{:S(2)}) copy-start(s32[8,12]{1,0:T(8,128)} %block_tile.5) | copy-start | bytes 1156
  259.2 4.1 %copy-start.1 = (s32[8,12]{1,0:T(8,128)S(1)}, s32[8,12]{1,0:T(8,128)}, u32[]{:S(2)}) copy-start(s32[8,12]{1,0:T(8,128)} %param.9) | copy-start | bytes 1156
  259.2 83.7 %all-to-all-start = ((bf16[32,6,72,128]{3,2,1,0:T(8,128)(2,1)}), bf16[32,6,72,128]{3,2,1,0:T(8,128)(2,1)}, u32[]{:S(2)}, u32[]{:S(2)}) async-start(bf16[32,6,72,128]{3,2,1,0:T(8,128)(2,1)} %bitcast.39), calls=%async_computation | async-start | bytes 7077888 | tf_op jit(solution)/shard_map/all_to_all | solution.py:375

commit v4 on v3

--- a/solution.py
+++ b/solution.py
@@ -1,4 +1,5 @@
 import functools
+import math
 
 import jax
 import jax.numpy as jnp
@@ -39,6 +40,15 @@
     return pltpu.with_memory_space_constraint(array, pltpu.HBM)
 
 
+def block_groups(count):
+    groups, first = [], 0
+    while first < count:
+        size = min(1 + len(groups), 4, count - first)
+        groups.append((first, size))
+        first += size
+    return groups
+
+
 def send_body(
     first_tile,
     width,
@@ -49,6 +59,7 @@
     out,
     tile_s,
     corr_ref,
+    corr_rows,
     mix,
     obs_buf,
     pat_buf,
@@ -65,17 +76,19 @@
     beam_count, chan_count = out.shape[:2]
     beams = pattern.shape[1]
     tiles = pixels // chan_count // LANES
-    depth = obs_buf.shape[0]
+    groups = block_groups(blk_beam)
+    sides = out_buf.shape[0]
     lanes = width * LANES
     rows = 2 * chan_dev
     beam_row = lax.axis_index("beam")
 
-    def obs_copies(k, slot):
+    def obs_copies(number):
+        blocks = pl.ds(*groups[number])
         return [
             pltpu.make_async_copy(
-                obs.at[k, :, :, :, pl.ds((part * tiles + first_tile + w) * LANES, LANES)],
-                obs_buf.at[slot, part * width + w],
-                in_sem.at[slot, part * width + w],
+                obs.at[blocks, :, :, :, pl.ds((part * tiles + first_tile + w) * LANES, LANES)],
+                obs_buf.at[part * width + w, blocks],
+                in_sem.at[number, part * width + w],
             )
             for part in range(chan_count)
             for w in range(width)
@@ -97,10 +110,10 @@
     tile_copy = pltpu.make_async_copy(block_tile, tile_s, tile_sem)
     corr_copy = pltpu.make_async_copy(correction, corr_ref, corr_sem)
     corr_copy.start()
-    for copy in obs_copies(0, 0) + pat_copies + [tile_copy]:
+    for copy in obs_copies(0) + pat_copies + [tile_copy]:
         copy.start()
-    for k in range(1, depth):
-        for copy in obs_copies(k, k):
+    for number in range(1, len(groups)):
+        for copy in obs_copies(number):
             copy.start()
 
     identity = (
@@ -108,19 +121,17 @@
         == lax.broadcasted_iota(jnp.int32, (chan_dev, chan_dev), 1)
     ).astype(jnp.float32)
     corr_copy.wait()
-    columns = [
-        [
-            lax.dot_general(
-                identity,
-                corr_ref[d, t],
-                (((1,), (1,)), ((), ())),
-                precision=lax.Precision.HIGHEST,
-                preferred_element_type=jnp.float32,
-            )
-            for t in range(stokes_in)
-        ]
-        for d in range(beam_dev)
-    ]
+    for d in range(beam_dev):
+        for t in range(stokes_in):
+            row = (d * stokes_in + t) * 2
+            corr_rows[row : row + 2] = corr_ref[d, t]
+    columns = lax.dot_general(
+        identity,
+        corr_rows[...],
+        (((1,), (1,)), ((), ())),
+        precision=lax.Precision.HIGHEST,
+        preferred_element_type=jnp.float32,
+    )
     inner = stokes_in * beam_dev
     wide = (chan_dev, chan_dev * inner)
     offset = lax.broadcasted_iota(jnp.int32, wide, 1) - inner * lax.broadcasted_iota(jnp.int32, wide, 0)
@@ -129,7 +140,8 @@
         for s in range(2):
             block = jnp.zeros(wide, jnp.float32)
             for t in range(stokes_in):
-                block = jnp.where(offset == t * beam_dev + d, columns[d][t][:, s : s + 1], block)
+                column = (d * stokes_in + t) * 2 + s
+                block = jnp.where(offset == t * beam_dev + d, columns[:, column : column + 1], block)
             top = block.astype(jnp.bfloat16).astype(jnp.float32)
             high.append(top)
             low.append(block - top)
@@ -147,27 +159,27 @@
                 ].astype(jnp.float32)
 
     def block(k, carry):
-        slot = lax.rem(k, depth)
-        side = lax.rem(k, 2)
-        for copy in obs_copies(k, slot):
-            copy.wait()
-
-        @pl.when(k >= 2)
+        side = lax.rem(k, sides)
+
+        @pl.when(k >= sides)
         def _():
             for d in range(beam_dev):
                 out_copy(side, d, 0, 0).wait()
 
-        for part in range(chan_count):
-            for w in range(width):
-                observed = obs_buf[slot, part * width + w].reshape(-1, LANES)
-                mixed = jnp.dot(mix[...], observed, preferred_element_type=jnp.float32)
-                corrected = mixed[: beam_dev * rows] + mixed[beam_dev * rows :]
+        for first in range(0, chan_count * width, 2):
+            observed = jnp.concatenate(
+                [obs_buf[first + half, k].reshape(-1, LANES) for half in range(2)], axis=1
+            )
+            mixed = jnp.dot(mix[...], observed, preferred_element_type=jnp.float32)
+            corrected = mixed[: beam_dev * rows] + mixed[beam_dev * rows :]
+            for half in range(2):
+                part, w = (first + half) // width, (first + half) % width
                 for d in range(beam_dev):
                     weight = pat_wide[
-                        part * width + w, pl.ds(k * beams + beam_row * beam_dev + d, 1)
+                        first + half, pl.ds(k * beams + beam_row * beam_dev + d, 1)
                     ]
                     out_buf[side, d, part, :, w * LANES : (w + 1) * LANES] = (
-                        corrected[d * rows : (d + 1) * rows] * weight
+                        corrected[d * rows : (d + 1) * rows, half * LANES : (half + 1) * LANES] * weight
                     ).astype(jnp.bfloat16)
         for d in range(beam_dev):
             owner = tile_s[beam_row * beam_dev + d, k] // TILE_DEV
@@ -175,15 +187,13 @@
             count[owner] = rank + 1
             out_copy(side, d, owner, rank).start()
 
-        @pl.when(k + depth < blk_beam)
-        def _():
-            for copy in obs_copies(k + depth, slot):
-                copy.start()
-
         return carry
 
-    lax.fori_loop(0, blk_beam, block, 0)
-    for side in range(2):
+    for number, (first_block, size) in enumerate(groups):
+        for copy in obs_copies(number):
+            copy.wait()
+        lax.fori_loop(first_block, first_block + size, block, 0)
+    for side in range(min(sides, blk_beam)):
         for d in range(beam_dev):
             out_copy(side, d, 0, 0).wait()
 
@@ -193,7 +203,6 @@
     rows = chan_dev * 2
     lanes = width * LANES
     beams = pattern_t.shape[1]
-    depth = 4
     anywhere = pl.BlockSpec(memory_space=pltpu.HBM)
     return pl.pallas_call(
         functools.partial(send_body, first_tile, width),
@@ -208,17 +217,18 @@
         scratch_shapes=[
             pltpu.SMEM(block_tile.shape, jnp.int32),
             pltpu.VMEM(corr_t.shape, jnp.float32),
+            pltpu.VMEM((corr_t.size // chan_dev, chan_dev), jnp.float32),
             pltpu.VMEM((2 * beam_dev * rows, chan_dev * stokes_in * beam_dev), jnp.bfloat16),
             pltpu.VMEM(
-                (depth, chan_count * width, chan_dev, stokes_in, beam_dev, LANES), jnp.bfloat16
+                (chan_count * width, blk_beam, chan_dev, stokes_in, beam_dev, LANES), jnp.bfloat16
             ),
             pltpu.VMEM((chan_count, blk_beam, beams, lanes), jnp.bfloat16),
             pltpu.VMEM((chan_count * width, blk_beam * beams, LANES), jnp.float32),
-            pltpu.VMEM((2, beam_dev, chan_count, rows, lanes), jnp.bfloat16),
+            pltpu.VMEM((4, beam_dev, chan_count, rows, lanes), jnp.bfloat16),
             pltpu.SMEM((beam_count,), jnp.int32),
-            pltpu.SemaphoreType.DMA((depth, chan_count * width)),
+            pltpu.SemaphoreType.DMA((len(block_groups(blk_beam)), chan_count * width)),
             pltpu.SemaphoreType.DMA((chan_count,)),
-            pltpu.SemaphoreType.DMA((2, beam_dev)),
+            pltpu.SemaphoreType.DMA((4, beam_dev)),
             pltpu.SemaphoreType.DMA(()),
             pltpu.SemaphoreType.DMA(()),
         ],
@@ -248,7 +258,17 @@
     for side in range(pair):
         slot = step * pair + side
         columns = slice(side * lanes, (side + 1) * lanes)
-        total[:, columns] = jnp.zeros_like(total[:, columns])
+        first, last = start_s[slot], start_s[slot + 1]
+
+        @pl.when(first == last)
+        def _():
+            total[:, columns] = jnp.zeros_like(total[:, columns])
+
+        @pl.when(first < last)
+        def _():
+            entry_copy(first, 0, 0).wait()
+            for part in range(parts):
+                total[part * rows : (part + 1) * rows, columns] = blocks[first, part].astype(jnp.float32)
 
         def add(i, carry):
             entry_copy(i, 0, 0).wait()
@@ -256,7 +276,7 @@
                 total[part * rows : (part + 1) * rows, columns] += blocks[i, part].astype(jnp.float32)
             return carry
 
-        lax.fori_loop(start_s[slot], start_s[slot + 1], add, 0)
+        lax.fori_loop(first + 1, last, add, 0)
     tiles = lanes // LANES
     sky = jnp.concatenate(
         [
@@ -266,14 +286,20 @@
         ],
         axis=1,
     ).astype(jnp.bfloat16)
-    spectrum = jnp.dot(table_ref[...], sky, preferred_element_type=jnp.float32)
-    for side in range(pair):
-        out_ref[side] = spectrum[:, side * lanes : (side + 1) * lanes].astype(out_ref.dtype)
+    piece = math.gcd(table_ref.shape[0], 256)
+    for first in range(0, table_ref.shape[0], piece):
+        spectrum = jnp.dot(
+            table_ref[first : first + piece], sky, preferred_element_type=jnp.float32
+        )
+        for side in range(pair):
+            out_ref[side, first : first + piece] = spectrum[
+                :, side * lanes : (side + 1) * lanes
+            ].astype(out_ref.dtype)
 
 
 def sky_chunk(recv, inverse, table, order, start, first_tile, width, tiles, earlier):
-    pair = 4
     slots = inverse.shape[1]
+    pair = math.gcd(slots, 5)
     lanes = width * LANES
     beam_count, parts, capacity, rows = recv.shape[:4]
     anywhere = pl.BlockSpec(memory_space=pltpu.HBM)

time: 353 us -> 352 us (level)
  no operation moved by 1% of the time
where the time goes in v4:
time: 352 us
  waiting for transfers between devices  253 us (72%)
  Pallas kernels  68.3 us (19%)
  starting transfers between devices  15.4 us (4%)
  local copies, waits for them, and re-layouts  7.58 us (2%)
  other arithmetic  6.6 us (2%)
    all_to_all x3, waiting for transfers between devices, shards(): lax.all_to_all(sent.reshape((beam_count * chan_count,) + sent.shape[2:]),...  253 us
    pallas_call x3, Pallas kernels, send_chunk(): pl.pallas_call(functools.partial(send_body, first_tile, width), out_shape...  35.2 us
    pallas_call x3, Pallas kernels, sky_chunk(): pl.pallas_call(functools.partial(sky_body, pair, first_tile), out_shape=j...  33.1 us
    all_to_all x3, starting transfers between devices, shards(): lax.all_to_all(sent.reshape((beam_count * chan_count,) + sent.shape[2:]),...  15.4 us
  transfers between devices with their start and end apart: 3, of which 3 were waited for; matrix products, arithmetic and copies ran while one was open for 4% of the time, Pallas kernels for 14%

profile of v4, /device:TPU:0, one launch (start us, length us, event | category | flops | bytes accessed | tf_op | source)
XLA Modules:
  0.0 351.9 jit_solution(1820032213056430018)
XLA Ops:
  0.0 9.8 %send_tile_0.1 = bf16[4,8,6,72,128]{4,3,2,1,0:T(8,128)(2,1)} custom-call(bf16[12,36,3,2,4096]{4,3,2,1,0:T(2,128)(2,1)} %bitcast.35, bf16[12,8,4096]{2,1,0:T(8,128)(2,1)} %bitcast.41, s32[8,12]{1,0:T(8,128)} %block_tile.5, f32[2,3,2,36]{3,2,1,0:T(2,128)} %bitcast.44), custom_call_target="tpu_custom_call" | custom-call | tf_op jit(solution)/shard_map/send_tile_0/pallas_call | solution.py:207
  9.8 7.4 %all-to-all-start.2 = ((bf16[32,6,72,128]{3,2,1,0:T(8,128)(2,1)}), bf16[32,6,72,128]{3,2,1,0:T(8,128)(2,1)}, u32[]{:S(2)}, u32[]{:S(2)}) async-start(bf16[32,6,72,128]{3,2,1,0:T(8,128)(2,1)} %bitcast.40), calls=%async_computation.2 | async-start | bytes 7077888 | tf_op jit(solution)/shard_map/all_to_all | solution.py:401
  17.2 15.6 %send_tile_1.1 = bf16[4,8,6,72,256]{4,3,2,1,0:T(8,128)(2,1)} custom-call(bf16[12,36,3,2,4096]{4,3,2,1,0:T(2,128)(2,1)} %bitcast.36, bf16[12,8,4096]{2,1,0:T(8,128)(2,1)} %bitcast.42, s32[8,12]{1,0:T(8,128)} %block_tile.5, f32[2,3,2,36]{3,2,1,0:T(2,128)} %bitcast.45), custom_call_target="tpu_custom_call" | custom-call | tf_op jit(solution)/shard_map/send_tile_1/pallas_call | solution.py:207
  32.8 64.2 %all-to-all-done.2 = bf16[32,6,72,128]{3,2,1,0:T(8,128)(2,1)} async-done(((bf16[32,6,72,128]{3,2,1,0:T(8,128)(2,1)}), bf16[32,6,72,128]{3,2,1,0:T(8,128)(2,1)}, u32[]{:S(2)}, u32[]{:S(2)}) %all-to-all-start.2) | async-done | bytes 3538976 | tf_op jit(solution)/shard_map/all_to_all | solution.py:401
  97.0 4.1 %all-to-all-start.1 = ((bf16[32,6,72,256]{3,2,1,0:T(8,128)(2,1)}), bf16[32,6,72,256]{3,2,1,0:T(8,128)(2,1)}, u32[]{:S(2)}, u32[]{:S(2)}) async-start(bf16[32,6,72,256]{3,2,1,0:T(8,128)(2,1)} %bitcast.38), calls=%async_computation.1 | async-start | bytes 14155776 | tf_op jit(solution)/shard_map/all_to_all | solution.py:401
  101.2 9.8 %send_tile_3.1 = bf16[4,8,6,72,128]{4,3,2,1,0:T(8,128)(2,1)} custom-call(bf16[12,36,3,2,4096]{4,3,2,1,0:T(2,128)(2,1)} %bitcast.37, bf16[12,8,4096]{2,1,0:T(8,128)(2,1)} %bitcast.43, s32[8,12]{1,0:T(8,128)} %block_tile.5, f32[2,3,2,36]{3,2,1,0:T(2,128)} %bitcast.46), custom_call_target="tpu_custom_call" | custom-call | tf_op jit(solution)/shard_map/send_tile_3/pallas_call | solution.py:207
  111.0 147.5 %all-to-all-done.1 = bf16[32,6,72,256]{3,2,1,0:T(8,128)(2,1)} async-done(((bf16[32,6,72,256]{3,2,1,0:T(8,128)(2,1)}), bf16[32,6,72,256]{3,2,1,0:T(8,128)(2,1)}, u32[]{:S(2)}, u32[]{:S(2)}) %all-to-all-start.1) | async-done | bytes 7077920 | tf_op jit(solution)/shard_map/all_to_all | solution.py:401
  258.5 0.0 copy-start
  258.5 0.0 copy-start.1
  258.5 3.9 %all-to-all-start = ((bf16[32,6,72,128]{3,2,1,0:T(8,128)(2,1)}), bf16[32,6,72,128]{3,2,1,0:T(8,128)(2,1)}, u32[]{:S(2)}, u32[]{:S(2)}) async-start(bf16[32,6,72,128]{3,2,1,0:T(8,128)(2,1)} %bitcast.39), calls=%async_computation | async-start | bytes 7077888 | tf_op jit(solution)/shard_map/all_to_all | solution.py:401
  262.4 0.0 copy-done
  262.4 0.1 copy.18
  262.6 0.1 eq.79
  262.7 0.0 copy-done.1
  262.7 0.1 copy.19
  262.8 0.1 copy.20
  262.9 0.2 convert_reduce_fusion
  263.0 0.2 select_reduce_fusion.1
  263.2 0.1 copy.21
  263.3 0.1 lt.78
  263.4 0.6 fusion.7
  264.7 2.4 multiply_sine_fusion
  267.1 0.3 pad_maximum_fusion
  267.4 1.1 reshape.200
  268.5 1.7 copy.24
  270.2 1.2 reshape.201
  271.4 2.7 copy.25
  274.1 0.9 convert_multiply_fusion
  275.0 0.1 copy.22
  275.2 0.1 eq.86
  275.3 0.2 fusion.1
  275.6 0.2 convert_reduce_fusion.2
  275.7 0.1 select_reduce_fusion
  275.9 0.1 convert_reduce_fusion.1.start_s
  276.0 1.6 fusion.table_ref
  277.6 9.4 %sky_tile_0.1.refs_0_ = bf16[20,1024,512]{2,1,0:T(8,128)(2,1)} custom-call(s32[2,24]{1,0:T(2,128)S(1)} %pad_add_fusion.order_s, s32[21]{0:T(128)S(1)} %convert_reduce_fusion.1.start_s, bf16[4,8,6,72,128]{4,3,2,1,0:T(8,128)(2,1)} %bitcast.16.recv, f32[4,20,128]{2,1,0:T(8,128)S(1)} %bitcast.32, bf16[1024,576]{1,0:T(8,128)(2,1)S(1)} %fusion.table_ref), custom_call_target="tpu_custom_call" | custom-call | tf_op jit(solution)/shard_map/sky_tile_0/pallas_call | solution.py:314
  287.0 14.2 %sky_tile_1.1.refs_0_ = bf16[20,1024,512]{2,1,0:T(8,128)(2,1)} custom-call(s32[2,24]{1,0:T(2,128)S(1)} %pad_add_fusion.order_s, s32[21]{0:T(128)S(1)} %convert_reduce_fusion.1.start_s, bf16[4,8,6,72,256]{4,3,2,1,0:T(8,128)(2,1)} %bitcast.14.recv, f32[4,20,128]{2,1,0:T(8,128)S(1)} %bitcast.33, ...), custom_call_target="tpu_custom_call", output_to_operand_aliasing={{}: (5, {})} | custom-call | tf_op jit(solution)/shard_map/sky_tile_1/pallas_call | solution.py:314
  301.3 41.0 %all-to-all-done = bf16[32,6,72,128]{3,2,1,0:T(8,128)(2,1)} async-done(((bf16[32,6,72,128]{3,2,1,0:T(8,128)(2,1)}), bf16[32,6,72,128]{3,2,1,0:T(8,128)(2,1)}, u32[]{:S(2)}, u32[]{:S(2)}) %all-to-all-start) | async-done | bytes 3538976 | tf_op jit(solution)/shard_map/all_to_all | solution.py:401
  342.2 9.5 %sky_tile_3.1 = bf16[20,1024,512]{2,1,0:T(8,128)(2,1)} custom-call(s32[2,24]{1,0:T(2,128)S(1)} %pad_add_fusion.order_s, s32[21]{0:T(128)S(1)} %convert_reduce_fusion.1.start_s, bf16[4,8,6,72,128]{4,3,2,1,0:T(8,128)(2,1)} %bitcast.11.recv, f32[4,20,128]{2,1,0:T(8,128)S(1)} %bitcast.34, ...), custom_call_target="tpu_custom_call", output_to_operand_aliasing={{}: (5, {})} | custom-call | tf_op jit(solution)/shard_map/sky_tile_3/pallas_call | solution.py:314
  (12 shorter events, 0.1 us)
Async XLA Ops:
  9.8 87.2 %all-to-all-start.2 = ((bf16[32,6,72,128]{3,2,1,0:T(8,128)(2,1)}), bf16[32,6,72,128]{3,2,1,0:T(8,128)(2,1)}, u32[]{:S(2)}, u32[]{:S(2)}) async-start(bf16[32,6,72,128]{3,2,1,0:T(8,128)(2,1)} %bitcast.40), calls=%async_computation.2 | async-start | bytes 7077888 | tf_op jit(solution)/shard_map/all_to_all | solution.py:401
  97.0 161.5 %all-to-all-start.1 = ((bf16[32,6,72,256]{3,2,1,0:T(8,128)(2,1)}), bf16[32,6,72,256]{3,2,1,0:T(8,128)(2,1)}, u32[]{:S(2)}, u32[]{:S(2)}) async-start(bf16[32,6,72,256]{3,2,1,0:T(8,128)(2,1)} %bitcast.38), calls=%async_computation.1 | async-start | bytes 14155776 | tf_op jit(solution)/shard_map/all_to_all | solution.py:401
  258.5 3.9 %copy-start = (s32[8,12]{1,0:T(8,128)S(1)}, s32[8,12]{1,0:T(8,128)}, u32[]{:S(2)}) copy-start(s32[8,12]{1,0:T(8,128)} %block_tile.5) | copy-start | bytes 1156
  258.5 4.1 %copy-start.1 = (s32[8,12]{1,0:T(8,128)S(1)}, s32[8,12]{1,0:T(8,128)}, u32[]{:S(2)}) copy-start(s32[8,12]{1,0:T(8,128)} %param.9) | copy-start | bytes 1156
  258.5 83.7 %all-to-all-start = ((bf16[32,6,72,128]{3,2,1,0:T(8,128)(2,1)}), bf16[32,6,72,128]{3,2,1,0:T(8,128)(2,1)}, u32[]{:S(2)}, u32[]{:S(2)}) async-start(bf16[32,6,72,128]{3,2,1,0:T(8,128)(2,1)} %bitcast.39), calls=%async_computation | async-start | bytes 7077888 | tf_op jit(solution)/shard_map/all_to_all | solution.py:401

commit v5 on v4

--- a/solution.py
+++ b/solution.py
@@ -43,7 +43,7 @@
 def block_groups(count):
     groups, first = [], 0
     while first < count:
-        size = min(1 + len(groups), 4, count - first)
+        size = min(2 + len(groups), 6, count - first)
         groups.append((first, size))
         first += size
     return groups
@@ -73,7 +73,7 @@
     corr_sem,
 ):
     blk_beam, chan_dev, stokes_in, beam_dev, pixels = obs.shape
-    beam_count, chan_count = out.shape[:2]
+    chan_count, beam_count = out.shape[:2]
     beams = pattern.shape[1]
     tiles = pixels // chan_count // LANES
     groups = block_groups(blk_beam)
@@ -96,7 +96,7 @@
 
     def out_copy(slot, d, owner, rank):
         return pltpu.make_async_copy(
-            out_buf.at[slot, d], out.at[owner, :, rank], out_sem.at[slot, d]
+            out_buf.at[slot, d], out.at[:, owner, rank], out_sem.at[slot, d]
         )
 
     pat_copies = [
@@ -206,7 +206,7 @@
     anywhere = pl.BlockSpec(memory_space=pltpu.HBM)
     return pl.pallas_call(
         functools.partial(send_body, first_tile, width),
-        out_shape=pltpu.HBM((beam_count, chan_count, CAP, rows, lanes), jnp.bfloat16),
+        out_shape=pltpu.HBM((chan_count, beam_count, CAP, rows, lanes), jnp.bfloat16),
         in_specs=[
             anywhere,
             anywhere,
@@ -245,7 +245,7 @@
     slots = pair * pl.num_programs(0)
 
     def entry_copy(i, source, rank):
-        return pltpu.make_async_copy(recv.at[source, :, rank], blocks.at[i], sem.at[i])
+        return pltpu.make_async_copy(recv.at[:, source, rank], blocks.at[i], sem.at[i])
 
     @pl.when(step == 0)
     def _():
@@ -301,7 +301,7 @@
     slots = inverse.shape[1]
     pair = math.gcd(slots, 5)
     lanes = width * LANES
-    beam_count, parts, capacity, rows = recv.shape[:4]
+    parts, beam_count, capacity, rows = recv.shape[:4]
     anywhere = pl.BlockSpec(memory_space=pltpu.HBM)
     whole = lambda a: pl.BlockSpec(a.shape, lambda l, *s: (0,) * a.ndim)
     in_specs = [anywhere, whole(inverse), whole(table)]
@@ -399,8 +399,8 @@
             obs_t, pattern_t, block_tile, corr_t, beam_count, chan_count, first_tile, width
         )
         received = lax.all_to_all(
-            sent.reshape((beam_count * chan_count,) + sent.shape[2:]),
-            ("beam", "chan"),
+            sent.reshape((chan_count * beam_count,) + sent.shape[2:]),
+            ("chan", "beam"),
             split_axis=0,
             concat_axis=0,
             tiled=True,

time: 352 us -> 351 us (level)
  waiting for transfers between devices: 253 us -> 247 us
  starting transfers between devices: 15.4 us -> 20.4 us
    all_to_all x3, waiting for transfers between devices: 253 us -> 247 us  [shards(): lax.all_to_all(sent.reshape((chan_count * beam_count,) + sent.shape[2:]),...]
    all_to_all x3, starting transfers between devices: 15.4 us -> 20.4 us  [shards(): lax.all_to_all(sent.reshape((chan_count * beam_count,) + sent.shape[2:]),...]
where the time goes in v5:
time: 351 us; the launch traced here: 350 us
  waiting for transfers between devices  247 us (70%)
  Pallas kernels  67.1 us (19%)
  starting transfers between devices  20.4 us (6%)
  local copies, waits for them, and re-layouts  7.58 us (2%)
  other arithmetic  6.6 us (2%)
    all_to_all x3, waiting for transfers between devices, shards(): lax.all_to_all(sent.reshape((chan_count * beam_count,) + sent.shape[2:]),...  247 us
    pallas_call x3, Pallas kernels, send_chunk(): pl.pallas_call(functools.partial(send_body, first_tile, width), out_shape...  34.6 us
    pallas_call x3, Pallas kernels, sky_chunk(): pl.pallas_call(functools.partial(sky_body, pair, first_tile), out_shape=j...  32.6 us
    all_to_all x3, starting transfers between devices, shards(): lax.all_to_all(sent.reshape((chan_count * beam_count,) + sent.shape[2:]),...  20.4 us
  transfers between devices with their start and end apart: 3, of which 3 were waited for; matrix products, arithmetic and copies ran while one was open for 4% of the time, Pallas kernels for 14%

profile of v5, /device:TPU:0, one launch (start us, length us, event | category | flops | bytes accessed | tf_op | source)
XLA Modules:
  0.0 350.1 jit_solution(4682607917097790737)
XLA Ops:
  0.0 9.6 %send_tile_0.1 = bf16[8,4,6,72,128]{4,3,2,1,0:T(8,128)(2,1)} custom-call(bf16[12,36,3,2,4096]{4,3,2,1,0:T(2,128)(2,1)} %bitcast.35, bf16[12,8,4096]{2,1,0:T(8,128)(2,1)} %bitcast.41, s32[8,12]{1,0:T(8,128)} %block_tile.5, f32[2,3,2,36]{3,2,1,0:T(2,128)} %bitcast.44), custom_call_target="tpu_custom_call" | custom-call | tf_op jit(solution)/shard_map/send_tile_0/pallas_call | solution.py:207
  9.7 7.4 %all-to-all-start.2 = ((bf16[32,6,72,128]{3,2,1,0:T(8,128)(2,1)}), bf16[32,6,72,128]{3,2,1,0:T(8,128)(2,1)}, u32[]{:S(2)}, u32[]{:S(2)}) async-start(bf16[32,6,72,128]{3,2,1,0:T(8,128)(2,1)} %bitcast.40), calls=%async_computation.2 | async-start | bytes 7077888 | tf_op jit(solution)/shard_map/all_to_all | solution.py:401
  17.0 15.3 %send_tile_1.1 = bf16[8,4,6,72,256]{4,3,2,1,0:T(8,128)(2,1)} custom-call(bf16[12,36,3,2,4096]{4,3,2,1,0:T(2,128)(2,1)} %bitcast.36, bf16[12,8,4096]{2,1,0:T(8,128)(2,1)} %bitcast.42, s32[8,12]{1,0:T(8,128)} %block_tile.5, f32[2,3,2,36]{3,2,1,0:T(2,128)} %bitcast.45), custom_call_target="tpu_custom_call" | custom-call | tf_op jit(solution)/shard_map/send_tile_1/pallas_call | solution.py:207
  32.3 63.2 %all-to-all-done.2 = bf16[32,6,72,128]{3,2,1,0:T(8,128)(2,1)} async-done(((bf16[32,6,72,128]{3,2,1,0:T(8,128)(2,1)}), bf16[32,6,72,128]{3,2,1,0:T(8,128)(2,1)}, u32[]{:S(2)}, u32[]{:S(2)}) %all-to-all-start.2) | async-done | bytes 3538976 | tf_op jit(solution)/shard_map/all_to_all | solution.py:401
  95.6 5.2 %all-to-all-start.1 = ((bf16[32,6,72,256]{3,2,1,0:T(8,128)(2,1)}), bf16[32,6,72,256]{3,2,1,0:T(8,128)(2,1)}, u32[]{:S(2)}, u32[]{:S(2)}) async-start(bf16[32,6,72,256]{3,2,1,0:T(8,128)(2,1)} %bitcast.38), calls=%async_computation.1 | async-start | bytes 14155776 | tf_op jit(solution)/shard_map/all_to_all | solution.py:401
  100.8 9.6 %send_tile_3.1 = bf16[8,4,6,72,128]{4,3,2,1,0:T(8,128)(2,1)} custom-call(bf16[12,36,3,2,4096]{4,3,2,1,0:T(2,128)(2,1)} %bitcast.37, bf16[12,8,4096]{2,1,0:T(8,128)(2,1)} %bitcast.43, s32[8,12]{1,0:T(8,128)} %block_tile.5, f32[2,3,2,36]{3,2,1,0:T(2,128)} %bitcast.46), custom_call_target="tpu_custom_call" | custom-call | tf_op jit(solution)/shard_map/send_tile_3/pallas_call | solution.py:207
  110.5 144.0 %all-to-all-done.1 = bf16[32,6,72,256]{3,2,1,0:T(8,128)(2,1)} async-done(((bf16[32,6,72,256]{3,2,1,0:T(8,128)(2,1)}), bf16[32,6,72,256]{3,2,1,0:T(8,128)(2,1)}, u32[]{:S(2)}, u32[]{:S(2)}) %all-to-all-start.1) | async-done | bytes 7077920 | tf_op jit(solution)/shard_map/all_to_all | solution.py:401
  254.5 0.0 copy-start
  254.5 0.0 copy-start.1
  254.5 7.8 %all-to-all-start = ((bf16[32,6,72,128]{3,2,1,0:T(8,128)(2,1)}), bf16[32,6,72,128]{3,2,1,0:T(8,128)(2,1)}, u32[]{:S(2)}, u32[]{:S(2)}) async-start(bf16[32,6,72,128]{3,2,1,0:T(8,128)(2,1)} %bitcast.39), calls=%async_computation | async-start | bytes 7077888 | tf_op jit(solution)/shard_map/all_to_all | solution.py:401
  262.3 0.0 copy-done
  262.3 0.1 copy.18
  262.5 0.1 eq.79
  262.6 0.0 copy-done.1
  262.6 0.1 copy.19
  262.7 0.1 copy.20
  262.8 0.2 convert_reduce_fusion
  262.9 0.2 select_reduce_fusion.1
  263.1 0.1 copy.21
  263.2 0.1 lt.78
  263.3 0.6 fusion.7
  264.6 2.4 multiply_sine_fusion
  267.0 0.3 pad_maximum_fusion
  267.3 1.1 reshape.200
  268.4 1.7 copy.24
  270.1 1.2 reshape.201
  271.3 2.7 copy.25
  274.0 0.9 convert_multiply_fusion
  274.9 0.1 copy.22
  275.1 0.1 eq.86
  275.2 0.2 fusion.1
  275.5 0.2 convert_reduce_fusion.2
  275.6 0.1 select_reduce_fusion
  275.8 0.1 convert_reduce_fusion.1.start_s
  275.9 1.6 fusion.table_ref
  277.5 9.3 %sky_tile_0.1.refs_0_ = bf16[20,1024,512]{2,1,0:T(8,128)(2,1)} custom-call(s32[2,24]{1,0:T(2,128)S(1)} %pad_add_fusion.order_s, s32[21]{0:T(128)S(1)} %convert_reduce_fusion.1.start_s, bf16[8,4,6,72,128]{4,3,2,1,0:T(8,128)(2,1)} %bitcast.16.recv, f32[4,20,128]{2,1,0:T(8,128)S(1)} %bitcast.32, bf16[1024,576]{1,0:T(8,128)(2,1)S(1)} %fusion.table_ref), custom_call_target="tpu_custom_call" | custom-call | tf_op jit(solution)/shard_map/sky_tile_0/pallas_call | solution.py:314
  286.8 14.0 %sky_tile_1.1.refs_0_ = bf16[20,1024,512]{2,1,0:T(8,128)(2,1)} custom-call(s32[2,24]{1,0:T(2,128)S(1)} %pad_add_fusion.order_s, s32[21]{0:T(128)S(1)} %convert_reduce_fusion.1.start_s, bf16[8,4,6,72,256]{4,3,2,1,0:T(8,128)(2,1)} %bitcast.14.recv, f32[4,20,128]{2,1,0:T(8,128)S(1)} %bitcast.33, ...), custom_call_target="tpu_custom_call", output_to_operand_aliasing={{}: (5, {})} | custom-call | tf_op jit(solution)/shard_map/sky_tile_1/pallas_call | solution.py:314
  300.8 39.9 %all-to-all-done = bf16[32,6,72,128]{3,2,1,0:T(8,128)(2,1)} async-done(((bf16[32,6,72,128]{3,2,1,0:T(8,128)(2,1)}), bf16[32,6,72,128]{3,2,1,0:T(8,128)(2,1)}, u32[]{:S(2)}, u32[]{:S(2)}) %all-to-all-start) | async-done | bytes 3538976 | tf_op jit(solution)/shard_map/all_to_all | solution.py:401
  340.6 9.3 %sky_tile_3.1 = bf16[20,1024,512]{2,1,0:T(8,128)(2,1)} custom-call(s32[2,24]{1,0:T(2,128)S(1)} %pad_add_fusion.order_s, s32[21]{0:T(128)S(1)} %convert_reduce_fusion.1.start_s, bf16[8,4,6,72,128]{4,3,2,1,0:T(8,128)(2,1)} %bitcast.11.recv, f32[4,20,128]{2,1,0:T(8,128)S(1)} %bitcast.34, ...), custom_call_target="tpu_custom_call", output_to_operand_aliasing={{}: (5, {})} | custom-call | tf_op jit(solution)/shard_map/sky_tile_3/pallas_call | solution.py:314
  (12 shorter events, 0.1 us)
Async XLA Ops:
  9.7 85.9 %all-to-all-start.2 = ((bf16[32,6,72,128]{3,2,1,0:T(8,128)(2,1)}), bf16[32,6,72,128]{3,2,1,0:T(8,128)(2,1)}, u32[]{:S(2)}, u32[]{:S(2)}) async-start(bf16[32,6,72,128]{3,2,1,0:T(8,128)(2,1)} %bitcast.40), calls=%async_computation.2 | async-start | bytes 7077888 | tf_op jit(solution)/shard_map/all_to_all | solution.py:401
  95.6 158.9 %all-to-all-start.1 = ((bf16[32,6,72,256]{3,2,1,0:T(8,128)(2,1)}), bf16[32,6,72,256]{3,2,1,0:T(8,128)(2,1)}, u32[]{:S(2)}, u32[]{:S(2)}) async-start(bf16[32,6,72,256]{3,2,1,0:T(8,128)(2,1)} %bitcast.38), calls=%async_computation.1 | async-start | bytes 14155776 | tf_op jit(solution)/shard_map/all_to_all | solution.py:401
  254.5 7.8 %copy-start = (s32[8,12]{1,0:T(8,128)S(1)}, s32[8,12]{1,0:T(8,128)}, u32[]{:S(2)}) copy-start(s32[8,12]{1,0:T(8,128)} %block_tile.5) | copy-start | bytes 1156
  254.5 8.1 %copy-start.1 = (s32[8,12]{1,0:T(8,128)S(1)}, s32[8,12]{1,0:T(8,128)}, u32[]{:S(2)}) copy-start(s32[8,12]{1,0:T(8,128)} %param.9) | copy-start | bytes 1156
  254.5 86.2 %all-to-all-start = ((bf16[32,6,72,128]{3,2,1,0:T(8,128)(2,1)}), bf16[32,6,72,128]{3,2,1,0:T(8,128)(2,1)}, u32[]{:S(2)}, u32[]{:S(2)}) async-start(bf16[32,6,72,128]{3,2,1,0:T(8,128)(2,1)} %bitcast.39), calls=%async_computation | async-start | bytes 7077888 | tf_op jit(solution)/shard_map/all_to_all | solution.py:401

commit v6 on v5

--- a/solution.py
+++ b/solution.py
@@ -286,7 +286,7 @@
         ],
         axis=1,
     ).astype(jnp.bfloat16)
-    piece = math.gcd(table_ref.shape[0], 256)
+    piece = math.gcd(table_ref.shape[0], 512)
     for first in range(0, table_ref.shape[0], piece):
         spectrum = jnp.dot(
             table_ref[first : first + piece], sky, preferred_element_type=jnp.float32
@@ -299,7 +299,7 @@
 
 def sky_chunk(recv, inverse, table, order, start, first_tile, width, tiles, earlier):
     slots = inverse.shape[1]
-    pair = math.gcd(slots, 5)
+    pair = math.gcd(slots, 10 if width == 1 else 5)
     lanes = width * LANES
     parts, beam_count, capacity, rows = recv.shape[:4]
     anywhere = pl.BlockSpec(memory_space=pltpu.HBM)

time: 351 us -> 351 us (level)
  no operation moved by 1% of the time
where the time goes in v6:
time: 351 us; the launch traced here: 350 us
  waiting for transfers between devices  248 us (71%)
  Pallas kernels  66.4 us (19%)
  starting transfers between devices  20.5 us (6%)
  local copies, waits for them, and re-layouts  7.58 us (2%)
  other arithmetic  6.6 us (2%)
    all_to_all x3, waiting for transfers between devices, shards(): lax.all_to_all(sent.reshape((chan_count * beam_count,) + sent.shape[2:]),...  248 us
    pallas_call x3, Pallas kernels, send_chunk(): pl.pallas_call(functools.partial(send_body, first_tile, width), out_shape...  34.5 us
    pallas_call x3, Pallas kernels, sky_chunk(): pl.pallas_call(functools.partial(sky_body, pair, first_tile), out_shape=j...  31.9 us
    all_to_all x3, starting transfers between devices, shards(): lax.all_to_all(sent.reshape((chan_count * beam_count,) + sent.shape[2:]),...  20.5 us
  transfers between devices with their start and end apart: 3, of which 3 were waited for; matrix products, arithmetic and copies ran while one was open for 4% of the time, Pallas kernels for 14%

profile of v6, /device:TPU:0, one launch (start us, length us, event | category | flops | bytes accessed | tf_op | source)
XLA Modules:
  0.0 349.9 jit_solution(17112772115412306908)
XLA Ops:
  0.0 9.6 %send_tile_0.1 = bf16[8,4,6,72,128]{4,3,2,1,0:T(8,128)(2,1)} custom-call(bf16[12,36,3,2,4096]{4,3,2,1,0:T(2,128)(2,1)} %bitcast.35, bf16[12,8,4096]{2,1,0:T(8,128)(2,1)} %bitcast.41, s32[8,12]{1,0:T(8,128)} %block_tile.5, f32[2,3,2,36]{3,2,1,0:T(2,128)} %bitcast.44), custom_call_target="tpu_custom_call" | custom-call | tf_op jit(solution)/shard_map/send_tile_0/pallas_call | solution.py:207
  9.6 7.4 %all-to-all-start.2 = ((bf16[32,6,72,128]{3,2,1,0:T(8,128)(2,1)}), bf16[32,6,72,128]{3,2,1,0:T(8,128)(2,1)}, u32[]{:S(2)}, u32[]{:S(2)}) async-start(bf16[32,6,72,128]{3,2,1,0:T(8,128)(2,1)} %bitcast.40), calls=%async_computation.2 | async-start | bytes 7077888 | tf_op jit(solution)/shard_map/all_to_all | solution.py:401
  17.1 15.3 %send_tile_1.1 = bf16[8,4,6,72,256]{4,3,2,1,0:T(8,128)(2,1)} custom-call(bf16[12,36,3,2,4096]{4,3,2,1,0:T(2,128)(2,1)} %bitcast.36, bf16[12,8,4096]{2,1,0:T(8,128)(2,1)} %bitcast.42, s32[8,12]{1,0:T(8,128)} %block_tile.5, f32[2,3,2,36]{3,2,1,0:T(2,128)} %bitcast.45), custom_call_target="tpu_custom_call" | custom-call | tf_op jit(solution)/shard_map/send_tile_1/pallas_call | solution.py:207
  32.4 63.2 %all-to-all-done.2 = bf16[32,6,72,128]{3,2,1,0:T(8,128)(2,1)} async-done(((bf16[32,6,72,128]{3,2,1,0:T(8,128)(2,1)}), bf16[32,6,72,128]{3,2,1,0:T(8,128)(2,1)}, u32[]{:S(2)}, u32[]{:S(2)}) %all-to-all-start.2) | async-done | bytes 3538976 | tf_op jit(solution)/shard_map/all_to_all | solution.py:401
  95.6 5.2 %all-to-all-start.1 = ((bf16[32,6,72,256]{3,2,1,0:T(8,128)(2,1)}), bf16[32,6,72,256]{3,2,1,0:T(8,128)(2,1)}, u32[]{:S(2)}, u32[]{:S(2)}) async-start(bf16[32,6,72,256]{3,2,1,0:T(8,128)(2,1)} %bitcast.38), calls=%async_computation.1 | async-start | bytes 14155776 | tf_op jit(solution)/shard_map/all_to_all | solution.py:401
  100.8 9.6 %send_tile_3.1 = bf16[8,4,6,72,128]{4,3,2,1,0:T(8,128)(2,1)} custom-call(bf16[12,36,3,2,4096]{4,3,2,1,0:T(2,128)(2,1)} %bitcast.37, bf16[12,8,4096]{2,1,0:T(8,128)(2,1)} %bitcast.43, s32[8,12]{1,0:T(8,128)} %block_tile.5, f32[2,3,2,36]{3,2,1,0:T(2,128)} %bitcast.46), custom_call_target="tpu_custom_call" | custom-call | tf_op jit(solution)/shard_map/send_tile_3/pallas_call | solution.py:207
  110.5 144.1 %all-to-all-done.1 = bf16[32,6,72,256]{3,2,1,0:T(8,128)(2,1)} async-done(((bf16[32,6,72,256]{3,2,1,0:T(8,128)(2,1)}), bf16[32,6,72,256]{3,2,1,0:T(8,128)(2,1)}, u32[]{:S(2)}, u32[]{:S(2)}) %all-to-all-start.1) | async-done | bytes 7077920 | tf_op jit(solution)/shard_map/all_to_all | solution.py:401
  254.5 0.0 copy-start
  254.5 0.0 copy-start.1
  254.5 7.8 %all-to-all-start = ((bf16[32,6,72,128]{3,2,1,0:T(8,128)(2,1)}), bf16[32,6,72,128]{3,2,1,0:T(8,128)(2,1)}, u32[]{:S(2)}, u32[]{:S(2)}) async-start(bf16[32,6,72,128]{3,2,1,0:T(8,128)(2,1)} %bitcast.39), calls=%async_computation | async-start | bytes 7077888 | tf_op jit(solution)/shard_map/all_to_all | solution.py:401
  262.3 0.0 copy-done
  262.4 0.1 copy.18
  262.5 0.1 eq.79
  262.6 0.0 copy-done.1
  262.6 0.1 copy.19
  262.7 0.1 copy.20
  262.8 0.2 convert_reduce_fusion
  263.0 0.2 select_reduce_fusion.1
  263.1 0.1 copy.21
  263.2 0.1 lt.78
  263.3 0.6 fusion.7
  264.6 2.4 multiply_sine_fusion
  267.0 0.3 pad_maximum_fusion
  267.3 1.1 reshape.200
  268.5 1.7 copy.24
  270.1 1.2 reshape.201
  271.3 2.7 copy.25
  274.1 0.9 convert_multiply_fusion
  275.0 0.1 copy.22
  275.1 0.1 eq.86
  275.2 0.2 fusion.1
  275.5 0.2 convert_reduce_fusion.2
  275.7 0.1 select_reduce_fusion
  275.8 0.1 convert_reduce_fusion.1.start_s
  276.0 1.6 fusion.table_ref
  277.5 8.9 %sky_tile_0.1.refs_0_ = bf16[20,1024,512]{2,1,0:T(8,128)(2,1)} custom-call(s32[2,24]{1,0:T(2,128)S(1)} %pad_add_fusion.order_s, s32[21]{0:T(128)S(1)} %convert_reduce_fusion.1.start_s, bf16[8,4,6,72,128]{4,3,2,1,0:T(8,128)(2,1)} %bitcast.16.recv, f32[4,20,128]{2,1,0:T(8,128)S(1)} %bitcast.32, bf16[1024,576]{1,0:T(8,128)(2,1)S(1)} %fusion.table_ref), custom_call_target="tpu_custom_call" | custom-call | tf_op jit(solution)/shard_map/sky_tile_0/pallas_call | solution.py:314
  286.4 14.0 %sky_tile_1.1.refs_0_ = bf16[20,1024,512]{2,1,0:T(8,128)(2,1)} custom-call(s32[2,24]{1,0:T(2,128)S(1)} %pad_add_fusion.order_s, s32[21]{0:T(128)S(1)} %convert_reduce_fusion.1.start_s, bf16[8,4,6,72,256]{4,3,2,1,0:T(8,128)(2,1)} %bitcast.14.recv, f32[4,20,128]{2,1,0:T(8,128)S(1)} %bitcast.33, ...), custom_call_target="tpu_custom_call", output_to_operand_aliasing={{}: (5, {})} | custom-call | tf_op jit(solution)/shard_map/sky_tile_1/pallas_call | solution.py:314
  300.4 40.3 %all-to-all-done = bf16[32,6,72,128]{3,2,1,0:T(8,128)(2,1)} async-done(((bf16[32,6,72,128]{3,2,1,0:T(8,128)(2,1)}), bf16[32,6,72,128]{3,2,1,0:T(8,128)(2,1)}, u32[]{:S(2)}, u32[]{:S(2)}) %all-to-all-start) | async-done | bytes 3538976 | tf_op jit(solution)/shard_map/all_to_all | solution.py:401
  340.7 9.1 %sky_tile_3.1 = bf16[20,1024,512]{2,1,0:T(8,128)(2,1)} custom-call(s32[2,24]{1,0:T(2,128)S(1)} %pad_add_fusion.order_s, s32[21]{0:T(128)S(1)} %convert_reduce_fusion.1.start_s, bf16[8,4,6,72,128]{4,3,2,1,0:T(8,128)(2,1)} %bitcast.11.recv, f32[4,20,128]{2,1,0:T(8,128)S(1)} %bitcast.34, ...), custom_call_target="tpu_custom_call", output_to_operand_aliasing={{}: (5, {})} | custom-call | tf_op jit(solution)/shard_map/sky_tile_3/pallas_call | solution.py:314
  (12 shorter events, 0.1 us)
Async XLA Ops:
  9.6 86.0 %all-to-all-start.2 = ((bf16[32,6,72,128]{3,2,1,0:T(8,128)(2,1)}), bf16[32,6,72,128]{3,2,1,0:T(8,128)(2,1)}, u32[]{:S(2)}, u32[]{:S(2)}) async-start(bf16[32,6,72,128]{3,2,1,0:T(8,128)(2,1)} %bitcast.40), calls=%async_computation.2 | async-start | bytes 7077888 | tf_op jit(solution)/shard_map/all_to_all | solution.py:401
  95.6 158.9 %all-to-all-start.1 = ((bf16[32,6,72,256]{3,2,1,0:T(8,128)(2,1)}), bf16[32,6,72,256]{3,2,1,0:T(8,128)(2,1)}, u32[]{:S(2)}, u32[]{:S(2)}) async-start(bf16[32,6,72,256]{3,2,1,0:T(8,128)(2,1)} %bitcast.38), calls=%async_computation.1 | async-start | bytes 14155776 | tf_op jit(solution)/shard_map/all_to_all | solution.py:401
  254.5 7.8 %copy-start = (s32[8,12]{1,0:T(8,128)S(1)}, s32[8,12]{1,0:T(8,128)}, u32[]{:S(2)}) copy-start(s32[8,12]{1,0:T(8,128)} %block_tile.5) | copy-start | bytes 1156
  254.5 8.1 %copy-start.1 = (s32[8,12]{1,0:T(8,128)S(1)}, s32[8,12]{1,0:T(8,128)}, u32[]{:S(2)}) copy-start(s32[8,12]{1,0:T(8,128)} %param.9) | copy-start | bytes 1156
  254.5 86.2 %all-to-all-start = ((bf16[32,6,72,128]{3,2,1,0:T(8,128)(2,1)}), bf16[32,6,72,128]{3,2,1,0:T(8,128)(2,1)}, u32[]{:S(2)}, u32[]{:S(2)}) async-start(bf16[32,6,72,128]{3,2,1,0:T(8,128)(2,1)} %bitcast.39), calls=%async_computation | async-start | bytes 7077888 | tf_op jit(solution)/shard_map/all_to_all | solution.py:401
